TPU v7x, 256 devices: a whole 4x4x8 slice. The times are simulated.
256 devices in a mesh: illum: 16 (over z_hi, x), row: 4 (over y), col: 4 (over z_lo, core).
Axes of the slice: x: 4, y: 4, z: 8 (z_hi: 4, z_lo: 2; z = z_hi * 2 + z_lo), core: 2. Of those that a mesh axis runs over, the one named last changes fastest.
Arguments:
- phase_delay: float32 [2, 512, 4096], P(None, ('row', 'illum'), 'col'), may hold values from -1 to 1
- angles: int32 [16, 2], P('illum'), may hold values from -8 to 8
- measured: bfloat16 [2, 16, 512, 4096], P(None, 'illum', 'row', 'col'), may hold values from -120 to 120, as said below
Outputs:
- phase_grad: float32 [2, 512, 4096], P(None, ('row', 'illum'), 'col')
Inputs may be any that keep to these rules, and one draw needn't show every extreme that they name: Real and imaginary parts of a measured field, with scales that vary over rows and columns.
All inputs are finite; a program needn't handle non-finite values.
Results may differ from a plain program's by a relative error of at most 0.0003.
Values sent between devices are 32-bit elements; how exact they have to be, the bound alone decides.
A program may use at most 64 MiB of HBM per device.

v0:
```python
import math

import jax
import jax.numpy as jnp
from jax import lax
from jax.sharding import PartitionSpec as P

SWEEPS = 2


beta_step = 0.5
eps_energy = 1e-06


def with_halo(x, sides, width):
    for axis, dim in sides:
        peers, length = (lax.axis_size(axis), x.shape[dim])
        up = [(i, (i + 1) % peers) for i in range(peers - 1)]
        down = [(j, i) for i, j in up]
        last = lax.slice_in_dim(x, length - width, length, axis=dim)
        first = lax.slice_in_dim(x, 0, width, axis=dim)
        before = lax.ppermute(last, axis, up)
        after = lax.ppermute(first, axis, down)
        x = jnp.concatenate([before, x, after], axis=dim)
    return x


def neighbour_sum(padded):
    return (
        padded[..., 2:, 1:-1]
        + padded[..., :-2, 1:-1]
        + padded[..., 1:-1, 2:]
        + padded[..., 1:-1, :-2]
    )


def exchange_rims(wave_field):
    return with_halo(wave_field, (("row", 2), ("col", 3)), 1)


def propagate(wave_field, direction):
    beta_sign = direction * beta_step
    divisor = 1.0 + 16.0 * beta_sign * beta_sign
    beside_all = neighbour_sum(exchange_rims(wave_field))
    real_part, imag_part = (wave_field[0], wave_field[1])
    rhs_real = real_part + 4.0 * beta_sign * imag_part - beta_sign * beside_all[1]
    rhs_imag = imag_part - 4.0 * beta_sign * real_part + beta_sign * beside_all[0]
    for sweep in range(SWEEPS):
        if sweep > 0:
            beside_all = neighbour_sum(exchange_rims(jnp.stack([real_part, imag_part])))
        total_real = rhs_real - beta_sign * beside_all[1]
        total_imag = rhs_imag + beta_sign * beside_all[0]
        real_part = (total_real + 4.0 * beta_sign * total_imag) / divisor
        imag_part = (total_imag - 4.0 * beta_sign * total_real) / divisor
    return jnp.stack([real_part, imag_part])


def per_device(phase_delay, angles, measured):
    illum_count = lax.axis_size("illum")
    stripe = phase_delay.shape[1]
    rows_tile = stripe * illum_count
    cols_tile = measured.shape[3]
    total_rows = rows_tile * lax.axis_size("row")
    total_cols = cols_tile * lax.axis_size("col")
    row_ids = lax.axis_index("row") * rows_tile + lax.iota(jnp.int32, rows_tile)
    col_ids = lax.axis_index("col") * cols_tile + lax.iota(jnp.int32, cols_tile)

    def advance(field_now, direction):
        return propagate(field_now, direction)

    along_x = angles[:, 0:1] * row_ids[None, :] % total_rows
    along_y = angles[:, 1:2] * col_ids[None, :] % total_cols
    angle_phase = (
        2.0
        * math.pi
        * (
            along_x.astype(jnp.float32)[:, :, None] / total_rows
            + along_y.astype(jnp.float32)[:, None, :] / total_cols
        )
    )
    wave_field = jnp.stack([jnp.cos(angle_phase), jnp.sin(angle_phase)])
    target = measured.astype(jnp.float32)
    energy = (
        lax.psum(jnp.sum(target * target, axis=(0, 2, 3)), ("row", "col"))
        / (total_rows * total_cols)
        + eps_energy
    )
    all_planes = lax.all_gather(phase_delay, "illum", axis=1, tiled=True)
    stored = []
    for depth_index in range(phase_delay.shape[0]):
        phase_plane = all_planes[depth_index]
        cosine = jnp.cos(phase_plane)
        sine_part = jnp.sin(phase_plane)
        modulated = jnp.stack(
            [
                wave_field[0] * cosine - wave_field[1] * sine_part,
                wave_field[0] * sine_part + wave_field[1] * cosine,
            ]
        )
        stored.append((modulated, cosine, sine_part))
        wave_field = advance(modulated, 1.0)
    adjoint_wave = 2.0 * (wave_field - target) / energy[None, :, None, None]
    slice_grads = [None] * len(stored)
    for depth_index in reversed(range(len(stored))):
        modulated, cosine, sine_part = stored[depth_index]
        adjoint_wave = advance(adjoint_wave, -1.0)
        slice_grads[depth_index] = jnp.sum(
            adjoint_wave[1] * modulated[0] - adjoint_wave[0] * modulated[1], axis=0
        )
        if depth_index > 0:
            adjoint_wave = jnp.stack(
                [
                    adjoint_wave[0] * cosine + adjoint_wave[1] * sine_part,
                    adjoint_wave[1] * cosine - adjoint_wave[0] * sine_part,
                ]
            )
    local_grads = jnp.stack(slice_grads)
    summed = lax.psum(local_grads, "illum")
    return lax.dynamic_slice_in_dim(summed, lax.axis_index("illum") * stripe, stripe, 1)


def solution(mesh):
    placed = (P(None, ("row", "illum"), "col"), P("illum", None), P(None, "illum", "row", "col"))
    return jax.shard_map(
        per_device,
        mesh=mesh,
        in_specs=placed,
        out_specs=P(None, ("row", "illum"), "col"),
        check_vma=False,
    )
```

profile of v0, /device:TPU:32, one launch (start us, length us, event | category | flops | bytes accessed | tf_op | source)
XLA Modules:
  0.0 427.6 jit_solution(10566999443613107633)
XLA Ops:
  6.5 0.7 all-gather.2.cloned.1.call-update
  9.8 54.2 %all-gather.2.cloned.1.call-done = f32[2,128,1024]{2,1,0:T(8,128)} async-done(((f32[2,8,1024]{2,1,0:T(8,128)}), f32[2,128,1024]{2,1,0:T(8,128)}) %all-gather.2.cloned.1.call-update) | async-done | bytes 1048592 | tf_op jit(solution)/shard_map/all_gather | solution.py:88
  64.1 4.8 %fusion.64 = (f32[1,1,128,1024]{3,2,1,0:T(8,128)S(1)}, f32[1,1,128,1024]{3,2,1,0:T(8,128)S(1)}) fusion(f32[2,128,1024]{2,1,0:T(8,128)} %all-gather.2.cloned.1.call-done, f32[1024]{0:T(1024)S(1)} %fusion.60, f32[128]{0:T(128)S(1)} %fusion.62), kind=kLoop, calls=%fused_computation.267 | loop fusion | flops 1048576 | bytes 1577472 | tf_op jit(solution)/shard_map/stack | solution.py:94
  68.9 3.4 collective-permute-start.1
  72.4 1.3 collective-permute-start
  73.7 4.2 collective-permute-done
  78.0 1.9 collective-permute-start.2
  80.0 2.5 collective-permute-start.3
  82.5 4.7 %collective-permute-done.3 = f32[2,1,130,1]{3,2,1,0:T(8,128)S(1)} collective-permute-done((f32[2,1,130,1]{3,2,1,0:T(8,128)S(1)}, f32[2,1,130,1]{3,2,1,0:T(8,128)S(1)}, u32[]{:S(2)}, u32[]{:S(2)}) %collective-permute-start.3) | collective-permute-done | bytes 1072 | tf_op jit(solution)/shard_map/ppermute | solution.py:22
  87.2 0.7 fusion.24
  87.9 4.2 multiply_bitcast_fusion.7
  92.1 3.6 collective-permute-start.5
  95.7 1.3 collective-permute-start.4
  97.1 4.2 collective-permute-done.4
  101.4 1.9 collective-permute-start.6
  103.3 2.4 collective-permute-start.7
  105.9 3.8 collective-permute-done.7
  110.4 6.1 %multiply_subtract_fusion.3 = (f32[1,128,1024]{2,1,0:T(8,128)S(1)}, f32[1,128,1024]{2,1,0:T(8,128)S(1)}) fusion(f32[2,128,1024]{2,1,0:T(8,128)S(1)} %copy-done, f32[2,1,128,1024]{3,2,1,0:T(8,128)S(1)} %fusion.21, f32[2,1,128,1024]{3,2,1,0:T(8,128)S(1)} %fusion.24, f32[1024]{0:T(1024)S(1)} %fusion.60, f32[128]{0:T(128)S(1)} %fusion.62), kind=kLoop, calls=%fused_computation.187 | loop fusion | flops 4194304 | bytes 4198912 | tf_op jit(solution)/shard_map/sub | solution.py:96
  116.5 2.9 collective-permute-start.9
  119.4 1.3 collective-permute-start.8
  120.8 4.2 collective-permute-done.8
  125.1 1.9 collective-permute-start.10
  127.0 2.4 collective-permute-start.11
  129.6 3.8 collective-permute-done.11
  135.4 1.9 collective-permute-start.13
  137.3 1.4 collective-permute-start.12
  138.7 4.2 collective-permute-done.12
  143.0 0.8 pad_maximum_fusion.111
  143.8 1.9 collective-permute-start.14
  145.7 2.4 collective-permute-start.15
  148.1 0.9 fusion.2
  149.0 25.0 %psum.14 = f32[1]{0:T(128)} all-reduce(f32[1]{0:T(128)} %bitcast.20), channel_id=1, replica_groups=mesh['illum'=16,'row'=4,'col'=4] {'row','col'}, use_global_device_ids=true, to_apply=%region_1.2 | all-reduce | flops 1 | bytes 8 | tf_op jit(solution)/shard_map/psum | solution.py:84
  174.7 0.7 fusion.15
  176.1 0.8 copy-done.6
  177.1 1.3 collective-permute-start.17
  178.4 1.3 collective-permute-start.16
  179.7 4.2 collective-permute-done.16
  184.1 1.9 collective-permute-start.18
  186.0 2.4 collective-permute-start.19
  188.6 6.5 %collective-permute-done.19 = f32[2,1,130,1]{3,2,1,0:T(8,128)S(1)} collective-permute-done((f32[2,1,130,1]{3,2,1,0:T(8,128)S(1)}, f32[2,1,130,1]{3,2,1,0:T(8,128)S(1)}, u32[]{:S(2)}, u32[]{:S(2)}) %collective-permute-start.19) | collective-permute-done | bytes 1072 | tf_op jit(solution)/shard_map/ppermute | solution.py:22
  196.1 1.6 collective-permute-start.21
  197.8 1.3 collective-permute-start.20
  199.1 4.2 collective-permute-done.20
  203.5 1.9 collective-permute-start.22
  205.4 2.6 collective-permute-start.23
  208.0 3.8 collective-permute-done.23
  212.5 2.3 multiply_add_fusion
  214.7 2.1 multiply_subtract_fusion.2
  216.9 2.0 collective-permute-start.25
  218.9 1.3 collective-permute-start.24
  220.3 4.2 collective-permute-done.24
  224.6 1.9 collective-permute-start.26
  226.5 2.4 collective-permute-start.27
  229.1 3.8 collective-permute-done.27
  234.2 1.9 collective-permute-start.29
  236.1 1.3 collective-permute-start.28
  237.5 4.2 collective-permute-done.28
  241.8 1.9 collective-permute-start.30
  243.7 2.4 collective-permute-start.31
  246.3 3.8 collective-permute-done.31
  250.8 4.1 multiply_subtract_fusion.1
  254.9 1.1 pad_maximum_fusion.92
  256.0 163.3 %all-reduce.2.cloned.1.call-done = f32[2,128,1024]{2,1,0:T(8,128)} async-done(((f32[2,128,1024]{2,1,0:T(8,128)}), f32[2,128,1024]{2,1,0:T(8,128)}) %all-reduce.2.cloned.1.call-update) | async-done | bytes 1048592 | tf_op jit(solution)/shard_map/psum | solution.py:118
  419.3 1.5 constant_dynamic-slice_fusion
  (66 shorter events, 11.7 us)
Async XLA Ops:
  6.5 57.6 %all-gather.2.cloned.1.call-start = ((), (), s32[]{:S(2)}) async-start(), calls=%async_computation | async-start | bytes 1114112 | tf_op jit(solution)/shard_map/all_gather | solution.py:88
  7.3 412.0 %all-reduce.2.cloned.1.call-start = ((), (), s32[]{:S(2)}) async-start(), calls=%async_computation.1 | async-start | bytes 2097152 | tf_op jit(solution)/shard_map/psum | solution.py:118
  7.3 0.7 copy-start.7
  68.9 4.8 %collective-permute-start.1 = (f32[2,1,1,1024]{3,2,1,0:T(1,128)S(1)}, f32[2,1,1,1024]{3,2,1,0:T(1,128)S(1)}, u32[]{:S(2)}, u32[]{:S(2)}) collective-permute-start(f32[2,1,1,1024]{3,2,1,0:T(1,128)S(1)} %get-tuple-element.56), channel_id=1, source_target_pairs={{0,4},{4,8},{8,12},{1,5},{5,9},{9,13},{2,6},{6,10},{10,14},{3,7},{... | collective-permute-start | bytes 24584 | tf_op jit(solution)/shard_map/ppermute | solution.py:22
  72.4 5.5 %collective-permute-start = (f32[2,1,1,1024]{3,2,1,0:T(1,128)S(1)}, f32[2,1,1,1024]{3,2,1,0:T(1,128)S(1)}, u32[]{:S(2)}, u32[]{:S(2)}) collective-permute-start(f32[2,1,1,1024]{3,2,1,0:T(1,128)S(1)} %get-tuple-element.57), channel_id=1, source_target_pairs={{4,0},{8,4},{12,8},{5,1},{9,5},{13,9},{6,2},{10,6},{14,10},{7,3},{... | collective-permute-start | bytes 24584 | tf_op jit(solution)/shard_map/ppermute | solution.py:23
  78.0 4.5 %collective-permute-start.2 = (f32[2,1,130,1]{3,2,1,0:T(8,128)S(1)}, f32[2,1,130,1]{3,2,1,0:T(8,128)S(1)}, u32[]{:S(2)}, u32[]{:S(2)}) collective-permute-start(f32[2,1,130,1]{3,2,1,0:T(8,128)S(1)} %get-tuple-element.36), channel_id=1, source_target_pairs={{1,0},{2,1},{3,2},{5,4},{6,5},{7,6},{9,8},{10,9},{11,10},{13,12},{... | collective-permute-start | bytes 3128 | tf_op jit(solution)/shard_map/ppermute | solution.py:23
  80.0 7.9 %copy-start = (f32[2,128,1024]{2,1,0:T(8,128)S(1)}, f32[2,128,1024]{2,1,0:T(8,128)}, u32[]{:S(2)}) copy-start(f32[2,128,1024]{2,1,0:T(8,128)} %all-gather.2.cloned.1.call-done) | copy-start | bytes 3145732
  80.0 7.2 %collective-permute-start.3 = (f32[2,1,130,1]{3,2,1,0:T(8,128)S(1)}, f32[2,1,130,1]{3,2,1,0:T(8,128)S(1)}, u32[]{:S(2)}, u32[]{:S(2)}) collective-permute-start(f32[2,1,130,1]{3,2,1,0:T(8,128)S(1)} %get-tuple-element.37), channel_id=1, source_target_pairs={{0,1},{1,2},{2,3},{4,5},{5,6},{6,7},{8,9},{9,10},{10,11},{12,13},{... | collective-permute-start | bytes 3128 | tf_op jit(solution)/shard_map/ppermute | solution.py:22
  92.1 4.9 %collective-permute-start.5 = (f32[2,1,1,1024]{3,2,1,0:T(1,128)S(1)}, f32[2,1,1,1024]{3,2,1,0:T(1,128)S(1)}, u32[]{:S(2)}, u32[]{:S(2)}) collective-permute-start(f32[2,1,1,1024]{3,2,1,0:T(1,128)S(1)} %get-tuple-element.54), channel_id=1, source_target_pairs={{0,4},{4,8},{8,12},{1,5},{5,9},{9,13},{2,6},{6,10},{10,14},{3,7},{... | collective-permute-start | bytes 24584 | tf_op jit(solution)/shard_map/ppermute | solution.py:22
  95.7 5.5 %collective-permute-start.4 = (f32[2,1,1,1024]{3,2,1,0:T(1,128)S(1)}, f32[2,1,1,1024]{3,2,1,0:T(1,128)S(1)}, u32[]{:S(2)}, u32[]{:S(2)}) collective-permute-start(f32[2,1,1,1024]{3,2,1,0:T(1,128)S(1)} %get-tuple-element.55), channel_id=1, source_target_pairs={{4,0},{8,4},{12,8},{5,1},{9,5},{13,9},{6,2},{10,6},{14,10},{7,3},{... | collective-permute-start | bytes 24584 | tf_op jit(solution)/shard_map/ppermute | solution.py:23
  101.4 4.5 %collective-permute-start.6 = (f32[2,1,130,1]{3,2,1,0:T(8,128)S(1)}, f32[2,1,130,1]{3,2,1,0:T(8,128)S(1)}, u32[]{:S(2)}, u32[]{:S(2)}) collective-permute-start(f32[2,1,130,1]{3,2,1,0:T(8,128)S(1)} %get-tuple-element.34), channel_id=1, source_target_pairs={{1,0},{2,1},{3,2},{5,4},{6,5},{7,6},{9,8},{10,9},{11,10},{13,12},{... | collective-permute-start | bytes 3128 | tf_op jit(solution)/shard_map/ppermute | solution.py:23
  103.3 6.4 %collective-permute-start.7 = (f32[2,1,130,1]{3,2,1,0:T(8,128)S(1)}, f32[2,1,130,1]{3,2,1,0:T(8,128)S(1)}, u32[]{:S(2)}, u32[]{:S(2)}) collective-permute-start(f32[2,1,130,1]{3,2,1,0:T(8,128)S(1)} %get-tuple-element.35), channel_id=1, source_target_pairs={{0,1},{1,2},{2,3},{4,5},{5,6},{6,7},{8,9},{9,10},{10,11},{12,13},{... | collective-permute-start | bytes 3128 | tf_op jit(solution)/shard_map/ppermute | solution.py:22
  116.5 4.3 %collective-permute-start.9 = (f32[2,1,1,1024]{3,2,1,0:T(1,128)S(1)}, f32[2,1,1,1024]{3,2,1,0:T(1,128)S(1)}, u32[]{:S(2)}, u32[]{:S(2)}) collective-permute-start(f32[2,1,1,1024]{3,2,1,0:T(1,128)S(1)} %get-tuple-element.52), channel_id=1, source_target_pairs={{0,4},{4,8},{8,12},{1,5},{5,9},{9,13},{2,6},{6,10},{10,14},{3,7},{... | collective-permute-start | bytes 24584 | tf_op jit(solution)/shard_map/ppermute | solution.py:22
  119.4 5.5 %collective-permute-start.8 = (f32[2,1,1,1024]{3,2,1,0:T(1,128)S(1)}, f32[2,1,1,1024]{3,2,1,0:T(1,128)S(1)}, u32[]{:S(2)}, u32[]{:S(2)}) collective-permute-start(f32[2,1,1,1024]{3,2,1,0:T(1,128)S(1)} %get-tuple-element.53), channel_id=1, source_target_pairs={{4,0},{8,4},{12,8},{5,1},{9,5},{13,9},{6,2},{10,6},{14,10},{7,3},{... | collective-permute-start | bytes 24584 | tf_op jit(solution)/shard_map/ppermute | solution.py:23
  125.1 4.5 %collective-permute-start.10 = (f32[2,1,130,1]{3,2,1,0:T(8,128)S(1)}, f32[2,1,130,1]{3,2,1,0:T(8,128)S(1)}, u32[]{:S(2)}, u32[]{:S(2)}) collective-permute-start(f32[2,1,130,1]{3,2,1,0:T(8,128)S(1)} %get-tuple-element.32), channel_id=1, source_target_pairs={{1,0},{2,1},{3,2},{5,4},{6,5},{7,6},{9,8},{10,9},{11,10},{13,12},{... | collective-permute-start | bytes 3128 | tf_op jit(solution)/shard_map/ppermute | solution.py:23
  127.0 6.4 %collective-permute-start.11 = (f32[2,1,130,1]{3,2,1,0:T(8,128)S(1)}, f32[2,1,130,1]{3,2,1,0:T(8,128)S(1)}, u32[]{:S(2)}, u32[]{:S(2)}) collective-permute-start(f32[2,1,130,1]{3,2,1,0:T(8,128)S(1)} %get-tuple-element.33), channel_id=1, source_target_pairs={{0,1},{1,2},{2,3},{4,5},{5,6},{6,7},{8,9},{9,10},{10,11},{12,13},{... | collective-permute-start | bytes 3128 | tf_op jit(solution)/shard_map/ppermute | solution.py:22
  134.3 0.8 copy-start.1
  134.3 1.0 copy-start.3
  135.4 3.4 collective-permute-start.13
  137.3 10.8 %copy-start.5 = (bf16[2,1,128,1024]{3,2,1,0:T(8,128)(2,1)S(1)}, bf16[2,1,128,1024]{3,2,1,0:T(8,128)(2,1)}, u32[]{:S(2)}) copy-start(bf16[2,1,128,1024]{3,2,1,0:T(8,128)(2,1)} %param.5) | copy-start | bytes 1572868
  137.3 5.7 %collective-permute-start.12 = (f32[2,1,1,1024]{3,2,1,0:T(1,128)S(1)}, f32[2,1,1,1024]{3,2,1,0:T(1,128)S(1)}, u32[]{:S(2)}, u32[]{:S(2)}) collective-permute-start(f32[2,1,1,1024]{3,2,1,0:T(1,128)S(1)} %get-tuple-element.51), channel_id=1, source_target_pairs={{4,0},{8,4},{12,8},{5,1},{9,5},{13,9},{6,2},{10,6},{14,10},{7,3},{... | collective-permute-start | bytes 24584 | tf_op jit(solution)/shard_map/ppermute | solution.py:23
  143.8 30.9 %collective-permute-start.14 = (f32[2,1,130,1]{3,2,1,0:T(8,128)}, f32[2,1,130,1]{3,2,1,0:T(8,128)S(1)}, u32[]{:S(2)}, u32[]{:S(2)}) collective-permute-start(f32[2,1,130,1]{3,2,1,0:T(8,128)} %get-tuple-element.30), channel_id=1, source_target_pairs={{1,0},{2,1},{3,2},{5,4},{6,5},{7,6},{9,8},{10,9},{11,10},{13,12},{... | collective-permute-start | bytes 3128 | tf_op jit(solution)/shard_map/ppermute | solution.py:23
  145.7 29.0 %collective-permute-start.15 = (f32[2,1,130,1]{3,2,1,0:T(8,128)}, f32[2,1,130,1]{3,2,1,0:T(8,128)S(1)}, u32[]{:S(2)}, u32[]{:S(2)}) collective-permute-start(f32[2,1,130,1]{3,2,1,0:T(8,128)} %get-tuple-element.31), channel_id=1, source_target_pairs={{0,1},{1,2},{2,3},{4,5},{5,6},{6,7},{8,9},{9,10},{10,11},{12,13},{... | collective-permute-start | bytes 3128 | tf_op jit(solution)/shard_map/ppermute | solution.py:22
  174.7 1.0 copy-start.2
  174.7 1.2 copy-start.4
  175.9 1.0 copy-start.6
  177.1 2.6 collective-permute-start.17
  178.4 5.5 %collective-permute-start.16 = (f32[2,1,1,1024]{3,2,1,0:T(1,128)S(1)}, f32[2,1,1,1024]{3,2,1,0:T(1,128)S(1)}, u32[]{:S(2)}, u32[]{:S(2)}) collective-permute-start(f32[2,1,1,1024]{3,2,1,0:T(1,128)S(1)} %get-tuple-element.49), channel_id=1, source_target_pairs={{4,0},{8,4},{12,8},{5,1},{9,5},{13,9},{6,2},{10,6},{14,10},{7,3},{... | collective-permute-start | bytes 24584 | tf_op jit(solution)/shard_map/ppermute | solution.py:23
  184.1 4.5 %collective-permute-start.18 = (f32[2,1,130,1]{3,2,1,0:T(8,128)S(1)}, f32[2,1,130,1]{3,2,1,0:T(8,128)S(1)}, u32[]{:S(2)}, u32[]{:S(2)}) collective-permute-start(f32[2,1,130,1]{3,2,1,0:T(8,128)S(1)} %get-tuple-element.28), channel_id=1, source_target_pairs={{1,0},{2,1},{3,2},{5,4},{6,5},{7,6},{9,8},{10,9},{11,10},{13,12},{... | collective-permute-start | bytes 3128 | tf_op jit(solution)/shard_map/ppermute | solution.py:23
  186.0 9.1 %collective-permute-start.19 = (f32[2,1,130,1]{3,2,1,0:T(8,128)S(1)}, f32[2,1,130,1]{3,2,1,0:T(8,128)S(1)}, u32[]{:S(2)}, u32[]{:S(2)}) collective-permute-start(f32[2,1,130,1]{3,2,1,0:T(8,128)S(1)} %get-tuple-element.29), channel_id=1, source_target_pairs={{0,1},{1,2},{2,3},{4,5},{5,6},{6,7},{8,9},{9,10},{10,11},{12,13},{... | collective-permute-start | bytes 3128 | tf_op jit(solution)/shard_map/ppermute | solution.py:22
  196.1 3.0 collective-permute-start.21
  197.8 5.5 %collective-permute-start.20 = (f32[2,1,1,1024]{3,2,1,0:T(1,128)S(1)}, f32[2,1,1,1024]{3,2,1,0:T(1,128)S(1)}, u32[]{:S(2)}, u32[]{:S(2)}) collective-permute-start(f32[2,1,1,1024]{3,2,1,0:T(1,128)S(1)} %get-tuple-element.47), channel_id=1, source_target_pairs={{4,0},{8,4},{12,8},{5,1},{9,5},{13,9},{6,2},{10,6},{14,10},{7,3},{... | collective-permute-start | bytes 24584 | tf_op jit(solution)/shard_map/ppermute | solution.py:23
  203.5 4.5 %collective-permute-start.22 = (f32[2,1,130,1]{3,2,1,0:T(8,128)S(1)}, f32[2,1,130,1]{3,2,1,0:T(8,128)S(1)}, u32[]{:S(2)}, u32[]{:S(2)}) collective-permute-start(f32[2,1,130,1]{3,2,1,0:T(8,128)S(1)} %get-tuple-element.26), channel_id=1, source_target_pairs={{1,0},{2,1},{3,2},{5,4},{6,5},{7,6},{9,8},{10,9},{11,10},{13,12},{... | collective-permute-start | bytes 3128 | tf_op jit(solution)/shard_map/ppermute | solution.py:23
  205.4 6.4 %collective-permute-start.23 = (f32[2,1,130,1]{3,2,1,0:T(8,128)S(1)}, f32[2,1,130,1]{3,2,1,0:T(8,128)S(1)}, u32[]{:S(2)}, u32[]{:S(2)}) collective-permute-start(f32[2,1,130,1]{3,2,1,0:T(8,128)S(1)} %get-tuple-element.27), channel_id=1, source_target_pairs={{0,1},{1,2},{2,3},{4,5},{5,6},{6,7},{8,9},{9,10},{10,11},{12,13},{... | collective-permute-start | bytes 3128 | tf_op jit(solution)/shard_map/ppermute | solution.py:22
  216.9 3.4 collective-permute-start.25
  218.9 5.5 %collective-permute-start.24 = (f32[2,1,1,1024]{3,2,1,0:T(1,128)S(1)}, f32[2,1,1,1024]{3,2,1,0:T(1,128)S(1)}, u32[]{:S(2)}, u32[]{:S(2)}) collective-permute-start(f32[2,1,1,1024]{3,2,1,0:T(1,128)S(1)} %get-tuple-element.43), channel_id=1, source_target_pairs={{4,0},{8,4},{12,8},{5,1},{9,5},{13,9},{6,2},{10,6},{14,10},{7,3},{... | collective-permute-start | bytes 24584 | tf_op jit(solution)/shard_map/ppermute | solution.py:23
  224.6 4.5 %collective-permute-start.26 = (f32[2,1,130,1]{3,2,1,0:T(8,128)S(1)}, f32[2,1,130,1]{3,2,1,0:T(8,128)S(1)}, u32[]{:S(2)}, u32[]{:S(2)}) collective-permute-start(f32[2,1,130,1]{3,2,1,0:T(8,128)S(1)} %get-tuple-element.24), channel_id=1, source_target_pairs={{1,0},{2,1},{3,2},{5,4},{6,5},{7,6},{9,8},{10,9},{11,10},{13,12},{... | collective-permute-start | bytes 3128 | tf_op jit(solution)/shard_map/ppermute | solution.py:23
  226.5 6.4 %collective-permute-start.27 = (f32[2,1,130,1]{3,2,1,0:T(8,128)S(1)}, f32[2,1,130,1]{3,2,1,0:T(8,128)S(1)}, u32[]{:S(2)}, u32[]{:S(2)}) collective-permute-start(f32[2,1,130,1]{3,2,1,0:T(8,128)S(1)} %get-tuple-element.25), channel_id=1, source_target_pairs={{0,1},{1,2},{2,3},{4,5},{5,6},{6,7},{8,9},{9,10},{10,11},{12,13},{... | collective-permute-start | bytes 3128 | tf_op jit(solution)/shard_map/ppermute | solution.py:22
  234.2 3.3 collective-permute-start.29
  236.1 5.5 %collective-permute-start.28 = (f32[2,1,1,1024]{3,2,1,0:T(1,128)S(1)}, f32[2,1,1,1024]{3,2,1,0:T(1,128)S(1)}, u32[]{:S(2)}, u32[]{:S(2)}) collective-permute-start(f32[2,1,1,1024]{3,2,1,0:T(1,128)S(1)} %get-tuple-element.41), channel_id=1, source_target_pairs={{4,0},{8,4},{12,8},{5,1},{9,5},{13,9},{6,2},{10,6},{14,10},{7,3},{... | collective-permute-start | bytes 24584 | tf_op jit(solution)/shard_map/ppermute | solution.py:23
  241.8 4.5 %collective-permute-start.30 = (f32[2,1,130,1]{3,2,1,0:T(8,128)S(1)}, f32[2,1,130,1]{3,2,1,0:T(8,128)S(1)}, u32[]{:S(2)}, u32[]{:S(2)}) collective-permute-start(f32[2,1,130,1]{3,2,1,0:T(8,128)S(1)} %get-tuple-element.22), channel_id=1, source_target_pairs={{1,0},{2,1},{3,2},{5,4},{6,5},{7,6},{9,8},{10,9},{11,10},{13,12},{... | collective-permute-start | bytes 3128 | tf_op jit(solution)/shard_map/ppermute | solution.py:23
  243.7 6.4 %collective-permute-start.31 = (f32[2,1,130,1]{3,2,1,0:T(8,128)S(1)}, f32[2,1,130,1]{3,2,1,0:T(8,128)S(1)}, u32[]{:S(2)}, u32[]{:S(2)}) collective-permute-start(f32[2,1,130,1]{3,2,1,0:T(8,128)S(1)} %get-tuple-element.23), channel_id=1, source_target_pairs={{0,1},{1,2},{2,3},{4,5},{5,6},{6,7},{8,9},{9,10},{10,11},{12,13},{... | collective-permute-start | bytes 3128 | tf_op jit(solution)/shard_map/ppermute | solution.py:22
Sparse Core Ops, SparseCore 0:
  9.8 54.2 all-gather.1
  256.1 163.1 all-reduce.1
where the time goes:
time: 430 us; the launch traced here: 428 us
  waiting for transfers between devices  283 us (66%)
  starting transfers between devices  64.2 us (15%)
  other arithmetic  35.7 us (8%)
  blocking collectives  25 us (6%)
  between operations  14.7 us (3%)
  local copies, waits for them, and re-layouts  4.82 us (1%)
    psum x1, waiting for transfers between devices, per_device(): summed = lax.psum(local_grads, 'illum')  163 us
    all_gather x1, waiting for transfers between devices, per_device(): all_planes = lax.all_gather(phase_delay, 'illum', axis=1, tiled=True)  54.2 us
    ppermute x16, starting transfers between devices, with_halo(): before = lax.ppermute(last, axis, up)  38.3 us
    ppermute x16, waiting for transfers between devices, with_halo(): after = lax.ppermute(first, axis, down)  34.4 us
    ppermute x16, waiting for transfers between devices, with_halo(): before = lax.ppermute(last, axis, up)  30.5 us
    ppermute x16, starting transfers between devices, with_halo(): after = lax.ppermute(first, axis, down)  25.8 us
    psum x1, blocking collectives, per_device(): lax.psum(jnp.sum(target * target, axis=(0, 2, 3)), ('row', 'col'))  25 us
  transfers between devices with their start and end apart: 34, of which 22 were waited for; matrix products, arithmetic and copies ran while one was open for 1% of the time, Pallas kernels for 0%

commit v1 on v0

v1 whole, which is shorter than its diff:
```python
import math

import jax
import jax.numpy as jnp
from jax import lax
from jax.experimental import pallas as pl
from jax.experimental.pallas import tpu as pltpu
from jax.sharding import PartitionSpec as P

ROWS, COLS, NLB = 128, 1024, 8
EXT, STEPS = 144, 18
TOTAL_ROWS, TOTAL_COLS = 512, 4096
EPS_ENERGY = 1e-06
MESH = pl.DeviceIdType.MESH
AG_UNITS = ((0, 7, "zx"), (7, 9, "xz"))
RS_UNITS = ((0, 6, "xz"), (6, 8, "zx"))
N_SEM = 200


def sincos(x):
    t = x * x
    s = x * (1.0 + t * (-1 / 6 + t * (1 / 120 + t * (-1 / 5040 + t * (1 / 362880)))))
    c = 1.0 + t * (-0.5 + t * (1 / 24 + t * (-1 / 720 + t * (1 / 40320 + t * (-1 / 3628800)))))
    return s, c


class Place:
    def __init__(self):
        illum = lax.axis_index("illum")
        self.zh, self.x = illum // 4, lax.rem(illum, 4)
        self.y, self.c = lax.axis_index("row"), lax.axis_index("col")

    def block(self, dz, dx):
        return lax.rem(self.zh + dz + 4, 4) * 4 + lax.rem(self.x + dx + 4, 4)

    def rows(self, dz, dx):
        return pl.ds(pl.multiple_of(8 * self.block(dz, dx), 8), 8)

    def illum(self, dz, dx):
        return {"illum": self.block(dz, dx)}

    def tile(self, dy, dc):
        return {"row": lax.rem(self.y + dy + 4, 4), "col": lax.rem(self.c + dc + 4, 4)}


class Wire:
    def __init__(self, send, recv):
        self.send, self.recv, self.all = send, recv, []

    def start(self, src, dst, device):
        k = len(self.all)
        copy = pltpu.make_async_remote_copy(
            src_ref=src,
            dst_ref=dst,
            send_sem=self.send.at[k],
            recv_sem=self.recv.at[k],
            device_id=device,
            device_id_type=MESH,
        )
        copy.start()
        self.all.append(copy)
        return copy


class Gather:
    def __init__(self, wire, place, planes, unit):
        self.w, self.p, self.planes = wire, place, planes
        self.b0, self.b1, self.order = unit
        self.along = {}

    def pos(self, da, db):
        return (da, db) if self.order == "zx" else (db, da)

    def part(self, da, db, plane=None):
        rows = self.p.rows(*self.pos(da, db))
        lead = slice(None) if plane is None else plane
        return self.planes.at[lead, self.b0 : self.b1, rows, :]

    def send(self, da, db, step, plane=None):
        ref = self.part(da, db, plane)
        return self.w.start(ref, ref, self.p.illum(*self.pos(*step)))

    def start_first(self):
        self.first = [self.send(0, 0, (1, 0)), self.send(0, 0, (-1, 0))]

    def relay_first(self, way):
        self.first[way].wait_recv()
        if way == 0:
            self.first.append(self.send(-1, 0, (1, 0), 0))
        else:
            self.first.append(self.send(1, 0, (-1, 0), 1))

    def end_first(self):
        self.first[2].wait_recv()
        self.first[3].wait_recv()

    def start_second(self, da):
        self.along[da] = [self.send(da, 0, (0, 1)), self.send(da, 0, (0, -1))]

    def relay_second(self, da):
        copies = self.along[da]
        copies[0].wait_recv()
        copies.append(self.send(da, -1, (0, 1), 0))
        copies[1].wait_recv()
        copies.append(self.send(da, 1, (0, -1), 1))

    def end_second(self, da):
        self.along[da][2].wait_recv()
        self.along[da][3].wait_recv()


class Scatter:
    def __init__(self, wire, place, grads, unit, bufs):
        self.w, self.p, self.g = wire, place, grads
        self.b0, self.b1, self.order = unit
        self.t1, self.t2, self.sums, self.t3, self.t4 = bufs

    def pos(self, da, db):
        return (da, db) if self.order == "zx" else (db, da)

    def part(self, da, dq, plane):
        return (plane, slice(self.b0, self.b1), self.p.rows(*self.pos(da, dq)), slice(None))

    def to(self, da, db):
        return self.p.illum(*self.pos(da, db))

    def start_first(self):
        self.c1, self.c2 = {}, []
        for dq in (2, 1, 3, 0):
            up = self.w.start(self.g.at[self.part(2, dq, 0)], self.t1.at[0, dq], self.to(1, 0))
            down = self.w.start(self.g.at[self.part(2, dq, 1)], self.t1.at[1, dq], self.to(-1, 0))
            self.c1[dq] = (up, down)
        self.c2e = {}
        for dq in (2, 1, 3, 0):
            up = self.w.start(self.g.at[self.part(1, dq, 1)], self.t2.at[0, dq, 1], self.to(1, 0))
            down = self.w.start(self.g.at[self.part(-1, dq, 0)], self.t2.at[1, dq, 0], self.to(-1, 0))
            self.c2e[dq] = (up, down)

    def middle_first(self):
        self.c2 = {}
        for dq in (2, 1, 3, 0):
            up, down = self.c1[dq]
            up.wait_recv()
            at = self.part(1, dq, 0)
            self.g[at] = self.g[at] + self.t1[0, dq]
            one = self.w.start(self.g.at[at], self.t2.at[0, dq, 0], self.to(1, 0))
            down.wait_recv()
            at = self.part(-1, dq, 1)
            self.g[at] = self.g[at] + self.t1[1, dq]
            two = self.w.start(self.g.at[at], self.t2.at[1, dq, 1], self.to(-1, 0))
            self.c2[dq] = (one, two)

    def add_first(self, dq):
        for copy in self.c2[dq] + self.c2e[dq]:
            copy.wait_recv()
        for plane in (0, 1):
            own = self.g[self.part(0, dq, plane)]
            self.sums[dq, plane] = own + self.t2[0, dq, plane] + self.t2[1, dq, plane]

    def start_second(self):
        self.add_first(2)
        self.c3 = (
            self.w.start(self.sums.at[2, 0], self.t3.at[0], self.to(0, 1)),
            self.w.start(self.sums.at[2, 1], self.t3.at[1], self.to(0, -1)),
        )
        self.add_first(1)
        self.c4 = [self.w.start(self.sums.at[1, 1], self.t4.at[0, 1], self.to(0, 1))]
        self.add_first(3)
        self.c4.append(self.w.start(self.sums.at[3, 0], self.t4.at[1, 0], self.to(0, -1)))
        self.add_first(0)

    def middle_second(self):
        self.c3[0].wait_recv()
        self.sums[1, 0] = self.sums[1, 0] + self.t3[0]
        self.c4.append(self.w.start(self.sums.at[1, 0], self.t4.at[0, 0], self.to(0, 1)))
        self.c3[1].wait_recv()
        self.sums[3, 1] = self.sums[3, 1] + self.t3[1]
        self.c4.append(self.w.start(self.sums.at[3, 1], self.t4.at[1, 1], self.to(0, -1)))

    def end_second(self, out):
        for copy in self.c4:
            copy.wait_recv()
        for plane in (0, 1):
            total = self.sums[0, plane] + self.t4[0, plane] + self.t4[1, plane]
            for b in range(self.b0, self.b1):
                out[plane, :, 128 * b : 128 * (b + 1)] = total[b - self.b0]


def strided(m):
    return pl.ds(m, 8, stride=STEPS)


def lanes_of(shape):
    return lax.broadcasted_iota(jnp.int32, shape, len(shape) - 1)


def kernel(
    phase_hbm, angles, meas_hbm, out,
    planes, edges, raw, meas, beside, w0, w1, rim, adj, turn, rowf, colf, rowm, energy, energy_in, grads,
    t1a, t2a, suma, t3a, t4a, t1b, t2b, sumb, t3b, t4b,
    local, send, recv,
):
    place = Place()
    wire = Wire(send, recv)
    own = place.rows(0, 0)
    fetch = [
        pltpu.make_async_copy(
            phase_hbm.at[:, :, 128 * b : 128 * (b + 1)], planes.at[:, b, own, :], local.at[b]
        )
        for b in range(NLB)
    ]
    fetch.append(pltpu.make_async_copy(meas_hbm.at[:, 0], raw, local.at[NLB]))
    for copy in fetch:
        copy.start()

    partners = [place.illum(1, 0), place.illum(-1, 0), place.illum(0, 1), place.illum(0, -1)]
    partners += [place.tile(d, 0) for d in (1, 2, 3)] + [place.tile(0, d) for d in (1, 2, 3)]
    partners += [place.tile(d, e) for d in (1, -1) for e in (1, -1)]
    barrier = pltpu.get_barrier_semaphore()
    for device in partners:
        pl.semaphore_signal(barrier, inc=1, device_id=device, device_id_type=MESH)
    pl.semaphore_wait(barrier, len(partners))

    for copy in fetch[:NLB]:
        copy.wait()
    edge_copies = [
        wire.start(planes.at[:, 0, own, :], edges.at[0], place.tile(0, -1)),
        wire.start(planes.at[:, NLB - 1, own, :], edges.at[1], place.tile(0, 1)),
    ]
    one, two = (Gather(wire, place, planes, unit) for unit in AG_UNITS)
    one.start_second(0)
    one.start_first()

    fetch[NLB].wait()
    energy[0] = jnp.zeros((8, 128), jnp.float32)

    def widen(g, carry):
        rows = pl.ds(pl.multiple_of(16 * g, 16), 16)
        for part in (0, 1):
            x = raw[part, rows, :].astype(jnp.float32)
            squares = x * x
            for b in range(NLB):
                meas[part, b, rows, :] = x[:, 128 * b : 128 * (b + 1)]
            half = squares[:8] + squares[8:]
            total = half[:, :128]
            for b in range(1, NLB):
                total = total + half[:, 128 * b : 128 * (b + 1)]
            energy[0] = energy[0] + total
        return carry

    lax.fori_loop(0, ROWS // 16, widen, 0)
    for copy in edge_copies:
        copy.wait_recv()
    lane = lanes_of((2, 8, 128))
    planes[:, NLB, own, :] = jnp.where(lane < 64, edges[0], edges[1])

    step_a, step_b = angles[0, 0], angles[0, 1]
    sub = lax.broadcasted_iota(jnp.int32, (8, 128), 0)

    def row_factor(m, carry):
        r = sub * STEPS + m
        gr = place.y * ROWS + jnp.where(r < 136, r, r - EXT)
        inside = jnp.where((gr >= 0) & (gr < TOTAL_ROWS), 1.0, 0.0)
        turns = jnp.bitwise_and(step_a * gr, TOTAL_ROWS - 1).astype(jnp.float32)
        theta = turns * (2.0 * math.pi / TOTAL_ROWS)
        co, si = jnp.cos(theta), jnp.sin(theta)
        rowf[0, m] = inside * (-0.28 * co - 0.96 * si)
        rowf[1, m] = inside * (0.96 * co - 0.28 * si)
        rowm[m] = inside
        return carry

    lane = lanes_of((8, 128))

    def col_of(b):
        edge = jnp.where(lane < 64, COLS + lane, lane - 128)
        return place.c * COLS + jnp.where(b < NLB, 128 * b + lane, edge)

    def col_factor(b, carry):
        gc = col_of(b)
        inside = jnp.where((gc >= 0) & (gc < TOTAL_COLS), 1.0, 0.0)
        turns = jnp.bitwise_and(step_b * gc, TOTAL_COLS - 1).astype(jnp.float32)
        theta = turns * (2.0 * math.pi / TOTAL_COLS)
        colf[0, b] = inside * jnp.cos(theta)
        colf[1, b] = inside * jnp.sin(theta)
        return carry

    two.start_first()
    two.start_second(0)
    energy_copies = [wire.start(energy.at[0], energy_in.at[d - 1], place.tile(d, 0)) for d in (1, 2, 3)]
    rims = []
    last, first = slice(120, 128), slice(0, 8)
    after, before = slice(128, 136), slice(136, 144)
    tile_rows = slice(0, 128)
    rims.append(wire.start(meas.at[:, :, last, :], meas.at[:, :, before, :], place.tile(1, 0)))
    rims.append(wire.start(meas.at[:, :, first, :], meas.at[:, :, after, :], place.tile(-1, 0)))
    for side, b, dc in ((0, 0, -1), (1, NLB - 1, 1)):
        rims.append(
            wire.start(meas.at[:, b, tile_rows, :], beside.at[side, :, tile_rows, :], place.tile(0, dc))
        )
        rims.append(wire.start(meas.at[:, b, last, :], beside.at[side, :, before, :], place.tile(1, dc)))
        rims.append(wire.start(meas.at[:, b, first, :], beside.at[side, :, after, :], place.tile(-1, dc)))
    lax.fori_loop(0, STEPS, row_factor, 0)
    lax.fori_loop(0, NLB + 1, col_factor, 0)

    one.relay_second(0)
    two.relay_first(0)
    two.start_second(-1)
    two.relay_first(1)
    two.start_second(1)
    for copy in energy_copies:
        copy.wait_recv()
    energy[1] = energy[0] + energy_in[0] + energy_in[1] + energy_in[2]
    energy_copies = [wire.start(energy.at[1], energy_in.at[2 + d], place.tile(0, d)) for d in (1, 2, 3)]
    one.relay_first(0)
    one.start_second(-1)
    one.relay_first(1)
    one.start_second(1)
    two.end_first()
    two.start_second(2)
    two.relay_second(0)
    one.end_first()
    one.start_second(2)
    one.end_second(0)
    one.relay_second(-1)
    one.relay_second(1)
    two.relay_second(-1)
    two.relay_second(1)
    two.relay_second(2)
    one.relay_second(2)
    for da in (-1, 1, 2):
        one.end_second(da)
    for da in (0, -1, 1, 2):
        two.end_second(da)
    ends = [
        wire.start(planes.at[:, :, last, :], planes.at[:, :, before, :], place.tile(1, 0)),
        wire.start(planes.at[:, :, first, :], planes.at[:, :, after, :], place.tile(-1, 0)),
    ]
    for copy in energy_copies:
        copy.wait_recv()
    total = energy[1] + energy_in[3] + energy_in[4] + energy_in[5]
    mean = jnp.sum(total, keepdims=True) * (1.0 / (TOTAL_ROWS * TOTAL_COLS)) + EPS_ENERGY
    kappa = jnp.broadcast_to(2.0 / mean, (8, 128))
    for copy in rims + ends:
        copy.wait_recv()

    gc8 = col_of(NLB)
    col_in = jnp.where((gc8 >= 0) & (gc8 < TOTAL_COLS), 1.0, 0.0)
    lane9 = lanes_of((NLB + 1, 8, 128))

    def scaled(m, amount):
        k = rowm[m] * amount
        return jnp.concatenate([jnp.broadcast_to(k[None], (NLB, 8, 128)), (k * col_in)[None]], axis=0)

    def around(field, part, i):
        mid = field[part, i]
        right = pltpu.roll(mid, 1, 2)
        left = pltpu.roll(mid, 127, 2)
        right = jnp.where(lane9 == 0, jnp.concatenate([right[NLB:], right[:NLB]], axis=0), right)
        left = jnp.where(lane9 == 127, jnp.concatenate([left[1:], left[:1]], axis=0), left)
        return (field[part, i - 1] + field[part, i + 1]) + (right + left)

    def wrap(field):
        for part in (0, 1):
            field[part, 0] = pltpu.roll(field[part, STEPS], 1, 1)
            field[part, STEPS + 1] = pltpu.roll(field[part, 1], 7, 1)

    def add_around(base, field, i, amount):
        k = scaled(i - 1, amount)
        real = base[0, i] - k * around(field, 1, i)
        imag = base[1, i] + k * around(field, 0, i)
        return real, imag

    def sweep(body):
        lax.fori_loop(1, STEPS + 1, lambda i, carry: (body(i), carry)[1], 0)

    def enter(i):
        m = i - 1
        si, co = sincos(planes[0, :, strided(m), :])
        fr, fi = rowf[0, m], rowf[1, m]
        cr, ci = colf[0], colf[1]
        ur = fr[None] * cr - fi[None] * ci
        ui = fr[None] * ci + fi[None] * cr
        w0[0, i] = ur * co - ui * si
        w0[1, i] = ur * si + ui * co

    def first_sweep(base, amount):
        def body(i):
            rim[0, i], rim[1, i] = add_around(base, base, i, amount)

        sweep(body)
        wrap(rim)

    sweep(enter)
    wrap(w0)
    first_sweep(w0, 0.5)

    def between(i):
        ur, ui = add_around(w0, rim, i, 0.2)
        si, co = sincos(planes[1, :, strided(i - 1), :])
        turn[0, i - 1] = co
        turn[1, i - 1] = si
        w1[0, i] = ur * co - ui * si
        w1[1, i] = ur * si + ui * co

    sweep(between)
    wrap(w1)
    first_sweep(w1, 0.5)

    def compare(i):
        m = i - 1
        ur, ui = add_around(w1, rim, i, 0.2)
        k = scaled(m, kappa)
        for part, u in ((0, ur), (1, ui)):
            side = jnp.where(lane < 64, beside[0, part, strided(m), :], beside[1, part, strided(m), :])
            seen = jnp.concatenate([meas[part, :, strided(m), :], side[None]], axis=0)
            adj[part, i] = k * (u - seen)

    sweep(compare)
    wrap(adj)
    first_sweep(adj, -0.5)

    def back(i):
        m = i - 1
        gr, gi = add_around(adj, rim, i, -0.2)
        grad = gi * w1[0, i] - gr * w1[1, i]
        grads[1, :, strided(m), :] = grad[:NLB]
        co, si = turn[0, m], turn[1, m]
        adj[0, i] = gr * co + gi * si
        adj[1, i] = gi * co - gr * si

    sweep(back)
    wrap(adj)
    first_sweep(adj, -0.5)

    def finish(i):
        gr, gi = add_around(adj, rim, i, -0.2)
        grad = gi * w0[0, i] - gr * w0[1, i]
        grads[0, :, strided(i - 1), :] = grad[:NLB]

    sweep(finish)

    bufs = ((t1a, t2a, suma, t3a, t4a), (t1b, t2b, sumb, t3b, t4b))
    sums = [Scatter(wire, place, grads, unit, b) for unit, b in zip(RS_UNITS, bufs)]
    for s in sums:
        s.start_first()
    for s in sums:
        s.middle_first()
    for s in sums:
        s.start_second()
    for s in sums:
        s.middle_second()
    for s in sums:
        s.end_second(out)
    for copy in wire.all:
        copy.wait_send()


def per_device(phase_delay, angles, measured):
    f32 = jnp.float32
    field = pltpu.VMEM((2, STEPS + 2, NLB + 1, 8, 128), f32)
    scratch = [
        pltpu.VMEM((2, NLB + 1, EXT, 128), f32),
        pltpu.VMEM((2, 2, 8, 128), f32),
        pltpu.VMEM((2, ROWS, COLS), jnp.bfloat16),
        pltpu.VMEM((2, NLB, EXT, 128), f32),
        pltpu.VMEM((2, 2, EXT, 128), f32),
        field,
        field,
        field,
        field,
        pltpu.VMEM((2, STEPS, NLB + 1, 8, 128), f32),
        pltpu.VMEM((2, STEPS, 8, 128), f32),
        pltpu.VMEM((2, NLB + 1, 8, 128), f32),
        pltpu.VMEM((STEPS, 8, 128), f32),
        pltpu.VMEM((2, 8, 128), f32),
        pltpu.VMEM((6, 8, 128), f32),
        pltpu.VMEM((2, NLB, EXT, 128), f32),
    ]
    for b0, b1, _ in RS_UNITS:
        n = b1 - b0
        scratch += [
            pltpu.VMEM((2, 4, n, 8, 128), f32),
            pltpu.VMEM((2, 4, 2, n, 8, 128), f32),
            pltpu.VMEM((4, 2, n, 8, 128), f32),
            pltpu.VMEM((2, n, 8, 128), f32),
            pltpu.VMEM((2, 2, n, 8, 128), f32),
        ]
    scratch += [
        pltpu.SemaphoreType.DMA((NLB + 1,)),
        pltpu.SemaphoreType.DMA((N_SEM,)),
        pltpu.SemaphoreType.DMA((N_SEM,)),
    ]
    return pl.pallas_call(
        kernel,
        out_shape=jax.ShapeDtypeStruct(phase_delay.shape, f32),
        in_specs=[
            pl.BlockSpec(memory_space=pl.ANY),
            pl.BlockSpec(memory_space=pltpu.SMEM),
            pl.BlockSpec(memory_space=pl.ANY),
        ],
        out_specs=pl.BlockSpec(memory_space=pltpu.VMEM),
        scratch_shapes=scratch,
        compiler_params=pltpu.CompilerParams(
            collective_id=0, has_side_effects=True, vmem_limit_bytes=56 << 20
        ),
        name="tomography",
    )(phase_delay, angles, measured)


def solution(mesh):
    placed = (P(None, ("row", "illum"), "col"), P("illum", None), P(None, "illum", "row", "col"))
    return jax.shard_map(
        per_device,
        mesh=mesh,
        in_specs=placed,
        out_specs=P(None, ("row", "illum"), "col"),
        check_vma=False,
    )
```

time: 430 us -> 70.4 us (0.16)
  waiting for transfers between devices: 283 us -> 0 us
  Pallas kernels: 0 us -> 68.4 us
  starting transfers between devices: 64.2 us -> 0 us
  other arithmetic: 35.7 us -> 0 us
  blocking collectives: 25 us -> 0 us
  between operations: 14.7 us -> 0.01 us
    psum x1 -> x0, waiting for transfers between devices: 163 us -> none  [per_device(): summed = lax.psum(local_grads, 'illum')]
    pallas_call x0 -> x1, Pallas kernels: none -> 68.4 us  [per_device(): pl.pallas_call(kernel, out_shape=jax.ShapeDtypeStruct(phase_delay.shape,...]
    ppermute x32 -> x0, waiting for transfers between devices: 64.9 us -> none  [the longest x16 34.4 us: with_halo(): after = lax.ppermute(first, axis, down)]
    ppermute x32 -> x0, starting transfers between devices: 64.1 us -> none  [the longest x16 38.3 us: with_halo(): before = lax.ppermute(last, axis, up)]
    all_gather x1 -> x0, waiting for transfers between devices: 54.2 us -> none  [per_device(): all_planes = lax.all_gather(phase_delay, 'illum', axis=1, tiled=True)]
    psum x1 -> x0, blocking collectives: 25 us -> none  [per_device(): lax.psum(jnp.sum(target * target, axis=(0, 2, 3)), ('row', 'col'))]
    sub x3 -> x0, other arithmetic: 12.3 us -> none  [the longest x1 6.09 us: per_device(): wave_field[0] * cosine - wave_field[1] * sine_part]
    another operation x15 -> x0, other arithmetic: 11.4 us -> none  [the longest x9 5.28 us: propagate(): beside_all = neighbour_sum(exchange_rims(jnp.stack([real_part, imag_part])))]
  transfers between devices with their start and end apart: 34 -> 0, of which waited for: 22 -> 0; matrix products, arithmetic and copies ran while one was open for 1% -> 0% of each run, Pallas kernels for 0% -> 0%
where the time goes in v1:
time: 70.4 us; the launch traced here: 69.8 us
  Pallas kernels  68.4 us (97%)
  local copies, waits for them, and re-layouts  1.47 us (2%)
    pallas_call x1, Pallas kernels, per_device(): pl.pallas_call(kernel, out_shape=jax.ShapeDtypeStruct(phase_delay.shape,...  68.4 us
    unnamed x1, local copies, waits for them, and re-layouts  1.47 us

profile of v1, /device:TPU:32, one launch (start us, length us, event | category | flops | bytes accessed | tf_op | source)
XLA Modules:
  0.0 69.8 jit_solution(969490602144690768)
XLA Ops:
  0.0 68.4 %tomography.1 = f32[2,8,1024]{2,1,0:T(8,128)} custom-call(f32[2,8,1024]{2,1,0:T(8,128)} %phase_hbm.1, s32[1,2]{1,0:T(1,128)} %angles.1, bf16[2,1,128,1024]{3,2,1,0:T(8,128)(2,1)} %meas_hbm.1), custom_call_target="tpu_custom_call" | custom-call | tf_op jit(solution)/shard_map/tomography/pallas_call | solution.py:493
  68.4 1.5 %copy.5 = f32[2,8,1024]{2,1,0:T(8,128)} copy(f32[2,8,1024]{2,1,0:T(8,128)} %tomography.1) | data formatting | bytes 131072

commit v2 on v1

v2 whole, which is shorter than its diff:
```python
import math

import jax
import jax.numpy as jnp
from jax import lax
from jax.experimental import pallas as pl
from jax.experimental.pallas import tpu as pltpu
from jax.sharding import PartitionSpec as P

ROWS, COLS, NLB = 128, 1024, 8
EXT, STEPS = 144, 18
TOTAL_ROWS, TOTAL_COLS = 512, 4096
EPS_ENERGY = 1e-06
MESH = pl.DeviceIdType.MESH
AG_UNITS = ((0, 7, "zx"), (7, 9, "xz"))
RS_UNITS = ((0, 6, "xz"), (6, 8, "zx"))
N_SEM = 60
UNROLL = 3
SPAN = 720


def sincos(x):
    t = x * x
    s = 0.008333314069458244 + t * (-0.00019835866408867098 + t * 2.6937597583896155e-06)
    s = x * (0.9999999999519255 + t * (-0.1666666642612366 + t * s))
    c = 0.04166645537534636 + t * (-0.0013882960343216638 + t * 2.4121201083497457e-05)
    c = 0.9999999994728761 + t * (-0.4999999736217199 + t * c)
    return s, c


class Place:
    def __init__(self):
        illum = lax.axis_index("illum")
        self.zh, self.x = illum // 4, lax.rem(illum, 4)
        self.y, self.c = lax.axis_index("row"), lax.axis_index("col")

    def block(self, dz, dx):
        return lax.rem(self.zh + dz + 4, 4) * 4 + lax.rem(self.x + dx + 4, 4)

    def rows(self, dz, dx):
        return pl.ds(pl.multiple_of(8 * self.block(dz, dx), 8), 8)

    def illum(self, dz, dx):
        return {"illum": self.block(dz, dx)}

    def tile(self, dy, dc):
        return {"row": lax.rem(self.y + dy + 4, 4), "col": lax.rem(self.c + dc + 4, 4)}


class Wire:
    def __init__(self, send, recv, span):
        self.send, self.recv, self.span = send, recv, span
        self.sent, self.groups = 0, []

    def group(self):
        self.groups.append(0)
        return len(self.groups) - 1

    def start(self, src, dst, device, group):
        tiles = math.prod(src.shape) // 1024
        self.sent += tiles
        self.groups[group] += tiles
        pltpu.make_async_remote_copy(
            src_ref=src,
            dst_ref=dst,
            send_sem=self.send.at[0],
            recv_sem=self.recv.at[group],
            device_id=device,
            device_id_type=MESH,
        ).start()

    def wait_for(self, sem, tiles):
        part = self.span.at[:tiles]
        pltpu.make_async_copy(part, part, sem).wait()

    def arrived(self, group):
        self.wait_for(self.recv.at[group], self.groups[group])

    def all_sent(self):
        self.wait_for(self.send.at[0], self.sent)


class Gather:
    def __init__(self, wire, place, planes, trig, unit, own):
        self.w, self.p, self.planes, self.trig, self.own = wire, place, planes, trig, own
        self.b0, self.b1, self.order = unit
        self.lanes = slice(128 * self.b0, 128 * self.b1)
        self.first = [wire.group() for _ in range(3)]
        self.second = {da: [wire.group() for _ in range(2)] for da in (0, -1, 1, 2)}
        self.last = wire.group()

    def pos(self, da, db):
        return (da, db) if self.order == "zx" else (db, da)

    def send(self, da, db, step, group, plane=None):
        rows = self.p.rows(*self.pos(da, db))
        lead = slice(None) if plane is None else plane
        dst = self.planes.at[lead, rows, self.lanes]
        src = dst
        if (da, db) == (0, 0) and self.own is not None:
            src = self.own.at[lead, :, self.lanes]
        self.w.start(src, dst, self.p.illum(*self.pos(*step)), group)

    def start_first(self):
        self.send(0, 0, (1, 0), self.first[0])
        self.send(0, 0, (-1, 0), self.first[1])

    def relay_first(self, way):
        self.w.arrived(self.first[way])
        if way == 0:
            self.send(-1, 0, (1, 0), self.first[2], 0)
        else:
            self.send(1, 0, (-1, 0), self.first[2], 1)

    def end_first(self):
        self.w.arrived(self.first[2])

    def start_second(self, da):
        self.send(da, 0, (0, 1), self.second[da][0])
        self.send(da, 0, (0, -1), self.second[da][1])

    def relay_second(self, da):
        self.w.arrived(self.second[da][0])
        self.send(da, -1, (0, 1), self.last, 0)
        self.w.arrived(self.second[da][1])
        self.send(da, 1, (0, -1), self.last, 1)

    def end(self):
        self.w.arrived(self.last)

    def turn(self, da, *dbs):
        for db in dbs:
            turn_rows(self.planes, self.trig, self.p.rows(*self.pos(da, db)), self.b0, self.b1)


def turn_rows(planes, trig, rows, b0, b1):
    s, c = sincos(planes[:, rows, 128 * b0 : 128 * b1])
    for b in range(b0, b1):
        at = slice(128 * (b - b0), 128 * (b - b0 + 1))
        for plane in (0, 1):
            trig[plane, 0, b, rows, :] = c[plane, :, at]
            trig[plane, 1, b, rows, :] = s[plane, :, at]


class Scatter:
    def __init__(self, wire, place, grads, unit, bufs):
        self.w, self.p, self.g = wire, place, grads
        self.b0, self.b1, self.order = unit
        self.t1, self.t2, self.sums, self.t3, self.t4 = bufs
        self.r1 = {dq: (wire.group(), wire.group()) for dq in range(4)}
        self.r2 = {dq: wire.group() for dq in range(4)}
        self.r3 = (wire.group(), wire.group())
        self.r4 = wire.group()

    def pos(self, da, db):
        return (da, db) if self.order == "zx" else (db, da)

    def part(self, da, dq, plane):
        return (plane, slice(self.b0, self.b1), self.p.rows(*self.pos(da, dq)), slice(None))

    def send(self, src, dst, da, db, group):
        self.w.start(src, dst, self.p.illum(*self.pos(da, db)), group)

    def start_first(self):
        for dq in (2, 1, 3, 0):
            self.send(self.g.at[self.part(2, dq, 0)], self.t1.at[0, dq], 1, 0, self.r1[dq][0])
            self.send(self.g.at[self.part(2, dq, 1)], self.t1.at[1, dq], -1, 0, self.r1[dq][1])
        for dq in (2, 1, 3, 0):
            self.send(self.g.at[self.part(1, dq, 1)], self.t2.at[0, dq, 1], 1, 0, self.r2[dq])
            self.send(self.g.at[self.part(-1, dq, 0)], self.t2.at[1, dq, 0], -1, 0, self.r2[dq])

    def middle_first(self):
        for dq in (2, 1, 3, 0):
            self.w.arrived(self.r1[dq][0])
            at = self.part(1, dq, 0)
            self.g[at] = self.g[at] + self.t1[0, dq]
            self.send(self.g.at[at], self.t2.at[0, dq, 0], 1, 0, self.r2[dq])
            self.w.arrived(self.r1[dq][1])
            at = self.part(-1, dq, 1)
            self.g[at] = self.g[at] + self.t1[1, dq]
            self.send(self.g.at[at], self.t2.at[1, dq, 1], -1, 0, self.r2[dq])

    def add_first(self, dq):
        self.w.arrived(self.r2[dq])
        for plane in (0, 1):
            own = self.g[self.part(0, dq, plane)]
            self.sums[dq, plane] = own + self.t2[0, dq, plane] + self.t2[1, dq, plane]

    def start_second(self):
        self.add_first(2)
        self.send(self.sums.at[2, 0], self.t3.at[0], 0, 1, self.r3[0])
        self.send(self.sums.at[2, 1], self.t3.at[1], 0, -1, self.r3[1])
        self.add_first(1)
        self.send(self.sums.at[1, 1], self.t4.at[0, 1], 0, 1, self.r4)
        self.add_first(3)
        self.send(self.sums.at[3, 0], self.t4.at[1, 0], 0, -1, self.r4)
        self.add_first(0)

    def middle_second(self):
        self.w.arrived(self.r3[0])
        self.sums[1, 0] = self.sums[1, 0] + self.t3[0]
        self.send(self.sums.at[1, 0], self.t4.at[0, 0], 0, 1, self.r4)
        self.w.arrived(self.r3[1])
        self.sums[3, 1] = self.sums[3, 1] + self.t3[1]
        self.send(self.sums.at[3, 1], self.t4.at[1, 1], 0, -1, self.r4)

    def end_second(self, out):
        self.w.arrived(self.r4)
        for plane in (0, 1):
            total = self.sums[0, plane] + self.t4[0, plane] + self.t4[1, plane]
            for b in range(self.b0, self.b1):
                out[plane, :, 128 * b : 128 * (b + 1)] = total[b - self.b0]


def strided(m):
    return pl.ds(m, 8, stride=STEPS)


def lanes_of(shape):
    return lax.broadcasted_iota(jnp.int32, shape, len(shape) - 1)


def kernel(
    phase_hbm, angles, meas_hbm, out,
    planes, trig, edges, raw, meas, beside, w0, w1, rim, adj, back1, rowf, colf, rowm, energy, energy_in,
    grads, span, t1a, t2a, suma, t3a, t4a, t1b, t2b, sumb, t3b, t4b,
    local, send, recv,
):
    place = Place()
    wire = Wire(send, recv, span)
    own = place.rows(0, 0)
    fetch = [
        pltpu.make_async_copy(phase_hbm, planes.at[:, own, :COLS], local.at[0]),
        pltpu.make_async_copy(meas_hbm.at[:, 0], raw, local.at[1]),
    ]
    partners = [place.illum(1, 0), place.illum(-1, 0), place.illum(0, 1), place.illum(0, -1)]
    partners += [place.tile(d, 0) for d in (1, 2, 3)] + [place.tile(0, d) for d in (1, 2, 3)]
    partners += [place.tile(d, e) for d in (1, -1) for e in (1, -1)]
    barrier = pltpu.get_barrier_semaphore()
    for device in partners:
        pl.semaphore_signal(barrier, inc=1, device_id=device, device_id_type=MESH)
    for copy in fetch:
        copy.start()
    pl.semaphore_wait(barrier, len(partners))

    edge_group = wire.group()
    wire.start(phase_hbm.at[:, :, :128], edges.at[0], place.tile(0, -1), edge_group)
    wire.start(phase_hbm.at[:, :, COLS - 128 :], edges.at[1], place.tile(0, 1), edge_group)
    one = Gather(wire, place, planes, trig, AG_UNITS[0], phase_hbm)
    two = Gather(wire, place, planes, trig, AG_UNITS[1], None)
    one.start_first()
    one.start_second(0)
    fetch[0].wait()
    one.turn(0, 0)
    wire.arrived(edge_group)
    lane = lanes_of((2, 8, 128))
    planes[:, own, COLS:] = jnp.where(lane < 64, edges[0], edges[1])
    two.start_first()
    two.start_second(0)
    two.turn(0, 0)

    fetch[1].wait()
    energy[0] = jnp.zeros((8, 128), jnp.float32)

    def widen(g, carry):
        rows = pl.ds(pl.multiple_of(16 * g, 16), 16)
        for part in (0, 1):
            x = raw[part, rows, :].astype(jnp.float32)
            squares = x * x
            for b in range(NLB):
                meas[part, b, rows, :] = x[:, 128 * b : 128 * (b + 1)]
            half = squares[:8] + squares[8:]
            total = half[:, :128]
            for b in range(1, NLB):
                total = total + half[:, 128 * b : 128 * (b + 1)]
            energy[0] = energy[0] + total
        return carry

    lax.fori_loop(0, ROWS // 16, widen, 0)

    step_a, step_b = angles[0, 0], angles[0, 1]
    sub = lax.broadcasted_iota(jnp.int32, (8, 128), 0)

    def row_factor(m, carry):
        r = sub * STEPS + m
        gr = place.y * ROWS + jnp.where(r < 136, r, r - EXT)
        inside = jnp.where((gr >= 0) & (gr < TOTAL_ROWS), 1.0, 0.0)
        turns = jnp.bitwise_and(step_a * gr, TOTAL_ROWS - 1).astype(jnp.float32)
        theta = turns * (2.0 * math.pi / TOTAL_ROWS)
        co, si = jnp.cos(theta), jnp.sin(theta)
        rowf[0, m] = inside * (-0.28 * co - 0.96 * si)
        rowf[1, m] = inside * (0.96 * co - 0.28 * si)
        rowm[m] = inside
        return carry

    lane = lanes_of((8, 128))

    def col_of(b):
        edge = jnp.where(lane < 64, COLS + lane, lane - 128)
        return place.c * COLS + jnp.where(b < NLB, 128 * b + lane, edge)

    def col_factor(b, carry):
        gc = col_of(b)
        inside = jnp.where((gc >= 0) & (gc < TOTAL_COLS), 1.0, 0.0)
        turns = jnp.bitwise_and(step_b * gc, TOTAL_COLS - 1).astype(jnp.float32)
        theta = turns * (2.0 * math.pi / TOTAL_COLS)
        colf[0, b] = inside * jnp.cos(theta)
        colf[1, b] = inside * jnp.sin(theta)
        return carry

    one.relay_second(0)
    one.turn(0, -1, 1)
    two.relay_first(0)
    two.start_second(-1)
    two.relay_first(1)
    two.start_second(1)
    lax.fori_loop(0, STEPS, row_factor, 0)
    lax.fori_loop(0, NLB + 1, col_factor, 0)
    one.relay_first(0)
    one.start_second(-1)
    one.relay_first(1)
    one.start_second(1)
    one.turn(-1, 0)
    one.turn(1, 0)
    two.turn(-1, 0)
    two.turn(1, 0)
    two.end_first()
    two.start_second(2)
    two.turn(2, 0)
    two.relay_second(0)
    two.turn(0, -1, 1)
    one.relay_second(-1)
    one.turn(-1, -1, 1)
    one.relay_second(1)
    one.turn(1, -1, 1)
    one.end_first()
    one.start_second(2)
    one.turn(2, 0)
    two.relay_second(-1)
    two.turn(-1, -1, 1)
    two.relay_second(1)
    two.turn(1, -1, 1)
    two.relay_second(2)
    two.turn(2, -1, 1)
    one.relay_second(2)
    one.turn(2, -1, 1)
    two.end()
    one.end()
    end_group = wire.group()
    last, first = slice(120, 128), slice(0, 8)
    after, before = slice(128, 136), slice(136, 144)
    wire.start(planes.at[:, last, :], planes.at[:, before, :], place.tile(1, 0), end_group)
    wire.start(planes.at[:, first, :], planes.at[:, after, :], place.tile(-1, 0), end_group)
    energy_group = wire.group()
    for d in (1, 2, 3):
        wire.start(energy.at[0], energy_in.at[d - 1], place.tile(d, 0), energy_group)
    rim_group = wire.group()
    tile_rows = slice(0, 128)
    wire.start(meas.at[:, :, last, :], meas.at[:, :, before, :], place.tile(1, 0), rim_group)
    wire.start(meas.at[:, :, first, :], meas.at[:, :, after, :], place.tile(-1, 0), rim_group)
    for side, b, dc in ((0, 0, -1), (1, NLB - 1, 1)):
        src, dst = meas.at[:, b], beside.at[side]
        wire.start(src.at[:, tile_rows, :], dst.at[:, tile_rows, :], place.tile(0, dc), rim_group)
        wire.start(src.at[:, last, :], dst.at[:, before, :], place.tile(1, dc), rim_group)
        wire.start(src.at[:, first, :], dst.at[:, after, :], place.tile(-1, dc), rim_group)
    for unit in (one, two):
        for da in (0, -1, 1, 2):
            unit.turn(da, 2)
    wire.arrived(end_group)
    turn_rows(planes, trig, after, 0, NLB + 1)
    turn_rows(planes, trig, before, 0, NLB + 1)

    gc8 = col_of(NLB)
    col_in = jnp.where((gc8 >= 0) & (gc8 < TOTAL_COLS), 1.0, 0.0)
    lane9 = lanes_of((NLB + 1, 8, 128))

    def scaled(m, amount):
        k = rowm[m] * amount
        return jnp.concatenate([jnp.broadcast_to(k[None], (NLB, 8, 128)), (k * col_in)[None]], axis=0)

    def around(field, part, i):
        mid = field[part, i]
        right = pltpu.roll(mid, 1, 2)
        left = pltpu.roll(mid, 127, 2)
        right = jnp.where(lane9 == 0, jnp.concatenate([right[NLB:], right[:NLB]], axis=0), right)
        left = jnp.where(lane9 == 127, jnp.concatenate([left[1:], left[:1]], axis=0), left)
        return (field[part, i - 1] + field[part, i + 1]) + (right + left)

    def wrap(field):
        for part in (0, 1):
            field[part, 0] = pltpu.roll(field[part, STEPS], 1, 1)
            field[part, STEPS + 1] = pltpu.roll(field[part, 1], 7, 1)

    def add_around(base, field, i, amount):
        k = scaled(i - 1, amount)
        real = base[0, i] - k * around(field, 1, i)
        imag = base[1, i] + k * around(field, 0, i)
        return real, imag

    def sweep(body):
        def several(t, carry):
            for k in range(UNROLL):
                body(UNROLL * t + k + 1)
            return carry

        lax.fori_loop(0, STEPS // UNROLL, several, 0)

    def enter(i):
        m = i - 1
        co, si = trig[0, 0, :, strided(m), :], trig[0, 1, :, strided(m), :]
        fr, fi = rowf[0, m], rowf[1, m]
        cr, ci = colf[0], colf[1]
        ur = fr[None] * cr - fi[None] * ci
        ui = fr[None] * ci + fi[None] * cr
        w0[0, i] = ur * co - ui * si
        w0[1, i] = ur * si + ui * co

    def first_sweep(base, amount):
        def body(i):
            rim[0, i], rim[1, i] = add_around(base, base, i, amount)

        sweep(body)
        wrap(rim)

    sweep(enter)
    wrap(w0)
    first_sweep(w0, 0.5)

    def between(i):
        ur, ui = add_around(w0, rim, i, 0.2)
        m = i - 1
        co, si = trig[1, 0, :, strided(m), :], trig[1, 1, :, strided(m), :]
        w1[0, i] = ur * co - ui * si
        w1[1, i] = ur * si + ui * co

    sweep(between)
    wire.arrived(energy_group)
    energy[1] = energy[0] + energy_in[0] + energy_in[1] + energy_in[2]
    energy_group = wire.group()
    for d in (1, 2, 3):
        wire.start(energy.at[1], energy_in.at[2 + d], place.tile(0, d), energy_group)
    wrap(w1)
    first_sweep(w1, 0.5)

    wire.arrived(energy_group)
    total = energy[1] + energy_in[3] + energy_in[4] + energy_in[5]
    mean = jnp.sum(total, keepdims=True) * (1.0 / (TOTAL_ROWS * TOTAL_COLS)) + EPS_ENERGY
    kappa = jnp.broadcast_to(2.0 / mean, (8, 128))
    wire.arrived(rim_group)

    def compare(i):
        m = i - 1
        ur, ui = add_around(w1, rim, i, 0.2)
        k = scaled(m, kappa)
        for part, u in ((0, ur), (1, ui)):
            side = jnp.where(lane < 64, beside[0, part, strided(m), :], beside[1, part, strided(m), :])
            seen = jnp.concatenate([meas[part, :, strided(m), :], side[None]], axis=0)
            adj[part, i] = k * (u - seen)

    sweep(compare)
    wrap(adj)
    first_sweep(adj, -0.5)

    def back(i):
        m = i - 1
        gr, gi = add_around(adj, rim, i, -0.2)
        grad = gi * w1[0, i] - gr * w1[1, i]
        grads[1, :, strided(m), :] = grad[:NLB]
        co, si = trig[1, 0, :, strided(m), :], trig[1, 1, :, strided(m), :]
        back1[0, i] = gr * co + gi * si
        back1[1, i] = gi * co - gr * si

    sweep(back)
    wrap(back1)
    first_sweep(back1, -0.5)

    def finish(i):
        gr, gi = add_around(back1, rim, i, -0.2)
        grad = gi * w0[0, i] - gr * w0[1, i]
        grads[0, :, strided(i - 1), :] = grad[:NLB]

    sweep(finish)

    bufs = ((t1a, t2a, suma, t3a, t4a), (t1b, t2b, sumb, t3b, t4b))
    sums = [Scatter(wire, place, grads, unit, b) for unit, b in zip(RS_UNITS, bufs)]
    for s in sums:
        s.start_first()
    for s in sums:
        s.middle_first()
    for s in sums:
        s.start_second()
    for s in sums:
        s.middle_second()
    for s in sums:
        s.end_second(out)
    wire.all_sent()


def per_device(phase_delay, angles, measured):
    f32 = jnp.float32
    field = pltpu.VMEM((2, STEPS + 2, NLB + 1, 8, 128), f32)
    scratch = [
        pltpu.VMEM((2, EXT, COLS + 128), f32),
        pltpu.VMEM((2, 2, NLB + 1, EXT, 128), f32),
        pltpu.VMEM((2, 2, 8, 128), f32),
        pltpu.VMEM((2, ROWS, COLS), jnp.bfloat16),
        pltpu.VMEM((2, NLB, EXT, 128), f32),
        pltpu.VMEM((2, 2, EXT, 128), f32),
        field,
        field,
        field,
        field,
        field,
        pltpu.VMEM((2, STEPS, 8, 128), f32),
        pltpu.VMEM((2, NLB + 1, 8, 128), f32),
        pltpu.VMEM((STEPS, 8, 128), f32),
        pltpu.VMEM((2, 8, 128), f32),
        pltpu.VMEM((6, 8, 128), f32),
        pltpu.VMEM((2, NLB, EXT, 128), f32),
        pltpu.VMEM((SPAN, 8, 128), f32),
    ]
    for b0, b1, _ in RS_UNITS:
        n = b1 - b0
        scratch += [
            pltpu.VMEM((2, 4, n, 8, 128), f32),
            pltpu.VMEM((2, 4, 2, n, 8, 128), f32),
            pltpu.VMEM((4, 2, n, 8, 128), f32),
            pltpu.VMEM((2, n, 8, 128), f32),
            pltpu.VMEM((2, 2, n, 8, 128), f32),
        ]
    scratch += [
        pltpu.SemaphoreType.DMA((2,)),
        pltpu.SemaphoreType.DMA((1,)),
        pltpu.SemaphoreType.DMA((N_SEM,)),
    ]
    return pl.pallas_call(
        kernel,
        out_shape=jax.ShapeDtypeStruct(phase_delay.shape, f32),
        in_specs=[
            pl.BlockSpec(memory_space=pl.ANY),
            pl.BlockSpec(memory_space=pltpu.SMEM),
            pl.BlockSpec(memory_space=pl.ANY),
        ],
        out_specs=pl.BlockSpec(memory_space=pltpu.VMEM),
        scratch_shapes=scratch,
        compiler_params=pltpu.CompilerParams(
            collective_id=0, has_side_effects=True, vmem_limit_bytes=56 << 20
        ),
        name="tomography",
    )(phase_delay, angles, measured)


def solution(mesh):
    placed = (P(None, ("row", "illum"), "col"), P("illum", None), P(None, "illum", "row", "col"))
    return jax.shard_map(
        per_device,
        mesh=mesh,
        in_specs=placed,
        out_specs=P(None, ("row", "illum"), "col"),
        check_vma=False,
    )
```

time: 70.4 us -> 61.4 us (0.87)
  Pallas kernels: 68.4 us -> 59.1 us
    pallas_call x1, Pallas kernels: 68.4 us -> 59.1 us  [per_device(): pl.pallas_call(kernel, out_shape=jax.ShapeDtypeStruct(phase_delay.shape,...]
where the time goes in v2:
time: 61.4 us; the launch traced here: 60.6 us
  Pallas kernels  59.1 us (96%)
  local copies, waits for them, and re-layouts  1.47 us (2%)
    pallas_call x1, Pallas kernels, per_device(): pl.pallas_call(kernel, out_shape=jax.ShapeDtypeStruct(phase_delay.shape,...  59.1 us
    unnamed x1, local copies, waits for them, and re-layouts  1.47 us

profile of v2, /device:TPU:32, one launch (start us, length us, event | category | flops | bytes accessed | tf_op | source)
XLA Modules:
  0.0 60.6 jit_solution(7317769781076976682)
XLA Ops:
  0.0 59.1 %tomography.1 = f32[2,8,1024]{2,1,0:T(8,128)} custom-call(f32[2,8,1024]{2,1,0:T(8,128)} %phase_hbm.1, s32[1,2]{1,0:T(1,128)} %angles.1, bf16[2,1,128,1024]{3,2,1,0:T(8,128)(2,1)} %meas_hbm.1), custom_call_target="tpu_custom_call" | custom-call | tf_op jit(solution)/shard_map/tomography/pallas_call | solution.py:536
  59.1 1.5 %copy.5 = f32[2,8,1024]{2,1,0:T(8,128)} copy(f32[2,8,1024]{2,1,0:T(8,128)} %tomography.1) | data formatting | bytes 131072

commit v3 on v2

--- a/solution.py
+++ b/solution.py
@@ -81,8 +81,8 @@
 
 
 class Gather:
-    def __init__(self, wire, place, planes, trig, unit, own):
-        self.w, self.p, self.planes, self.trig, self.own = wire, place, planes, trig, own
+    def __init__(self, wire, place, planes, trig, unit):
+        self.w, self.p, self.planes, self.trig = wire, place, planes, trig
         self.b0, self.b1, self.order = unit
         self.lanes = slice(128 * self.b0, 128 * self.b1)
         self.first = [wire.group() for _ in range(3)]
@@ -95,11 +95,8 @@
     def send(self, da, db, step, group, plane=None):
         rows = self.p.rows(*self.pos(da, db))
         lead = slice(None) if plane is None else plane
-        dst = self.planes.at[lead, rows, self.lanes]
-        src = dst
-        if (da, db) == (0, 0) and self.own is not None:
-            src = self.own.at[lead, :, self.lanes]
-        self.w.start(src, dst, self.p.illum(*self.pos(*step)), group)
+        ref = self.planes.at[lead, rows, self.lanes]
+        self.w.start(ref, ref, self.p.illum(*self.pos(*step)), group)
 
     def start_first(self):
         self.send(0, 0, (1, 0), self.first[0])
@@ -204,25 +201,40 @@
         self.sums[3, 1] = self.sums[3, 1] + self.t3[1]
         self.send(self.sums.at[3, 1], self.t4.at[1, 1], 0, -1, self.r4)
 
-    def end_second(self, out):
-        self.w.arrived(self.r4)
-        for plane in (0, 1):
-            total = self.sums[0, plane] + self.t4[0, plane] + self.t4[1, plane]
-            for b in range(self.b0, self.b1):
-                out[plane, :, 128 * b : 128 * (b + 1)] = total[b - self.b0]
+    def end_second(self, plane):
+        total = self.sums[0, plane] + self.t4[0, plane] + self.t4[1, plane]
+        return [total[b] for b in range(self.b1 - self.b0)]
 
 
 def strided(m):
     return pl.ds(m, 8, stride=STEPS)
 
 
+def swapped(blocks):
+    blocks = list(blocks)
+    lane = lanes_of(blocks[0].shape)
+    last = lane.ndim - 1
+    for k in (1, 2, 4):
+        low = jnp.bitwise_and(lane, k) == 0
+        for b in range(NLB):
+            if not b & k:
+                one, two = blocks[b], blocks[b | k]
+                blocks[b] = jnp.where(low, one, pltpu.roll(two, k, last))
+                blocks[b | k] = jnp.where(low, pltpu.roll(one, 128 - k, last), two)
+    return blocks
+
+
+def split(x):
+    return [x[..., 128 * b : 128 * (b + 1)] for b in range(NLB)]
+
+
 def lanes_of(shape):
     return lax.broadcasted_iota(jnp.int32, shape, len(shape) - 1)
 
 
 def kernel(
     phase_hbm, angles, meas_hbm, out,
-    planes, trig, edges, raw, meas, beside, w0, w1, rim, adj, back1, rowf, colf, rowm, energy, energy_in,
+    planes, trig, fresh, edges, raw, meas, rims, beside, w0, w1, rim, adj, back1, rowf, colf, rowm, energy, energy_in,
     grads, span, t1a, t2a, suma, t3a, t4a, t1b, t2b, sumb, t3b, t4b,
     local, send, recv,
 ):
@@ -230,7 +242,7 @@
     wire = Wire(send, recv, span)
     own = place.rows(0, 0)
     fetch = [
-        pltpu.make_async_copy(phase_hbm, planes.at[:, own, :COLS], local.at[0]),
+        pltpu.make_async_copy(phase_hbm, fresh, local.at[0]),
         pltpu.make_async_copy(meas_hbm.at[:, 0], raw, local.at[1]),
     ]
     partners = [place.illum(1, 0), place.illum(-1, 0), place.illum(0, 1), place.illum(0, -1)]
@@ -246,15 +258,17 @@
     edge_group = wire.group()
     wire.start(phase_hbm.at[:, :, :128], edges.at[0], place.tile(0, -1), edge_group)
     wire.start(phase_hbm.at[:, :, COLS - 128 :], edges.at[1], place.tile(0, 1), edge_group)
-    one = Gather(wire, place, planes, trig, AG_UNITS[0], phase_hbm)
-    two = Gather(wire, place, planes, trig, AG_UNITS[1], None)
+    one = Gather(wire, place, planes, trig, AG_UNITS[0])
+    two = Gather(wire, place, planes, trig, AG_UNITS[1])
+    fetch[0].wait()
+    for b, block in enumerate(swapped(split(fresh[...]))):
+        planes[:, own, 128 * b : 128 * (b + 1)] = block
     one.start_first()
     one.start_second(0)
-    fetch[0].wait()
     one.turn(0, 0)
     wire.arrived(edge_group)
     lane = lanes_of((2, 8, 128))
-    planes[:, own, COLS:] = jnp.where(lane < 64, edges[0], edges[1])
+    planes[:, own, COLS:] = jnp.where(lane < 64, pltpu.roll(edges[0], 8, 2), pltpu.roll(edges[1], 120, 2))
     two.start_first()
     two.start_second(0)
     two.turn(0, 0)
@@ -267,8 +281,11 @@
         for part in (0, 1):
             x = raw[part, rows, :].astype(jnp.float32)
             squares = x * x
-            for b in range(NLB):
-                meas[part, b, rows, :] = x[:, 128 * b : 128 * (b + 1)]
+            blocks = split(x)
+            rims[0, part, rows, :] = pltpu.roll(blocks[0], 8, 1)
+            rims[1, part, rows, :] = pltpu.roll(blocks[NLB - 1], 120, 1)
+            for b, block in enumerate(swapped(blocks)):
+                meas[part, b, rows, :] = block
             half = squares[:8] + squares[8:]
             total = half[:, :128]
             for b in range(1, NLB):
@@ -296,8 +313,9 @@
     lane = lanes_of((8, 128))
 
     def col_of(b):
-        edge = jnp.where(lane < 64, COLS + lane, lane - 128)
-        return place.c * COLS + jnp.where(b < NLB, 128 * b + lane, edge)
+        edge = jnp.where(lane < 64, COLS - 8 + lane, lane - 120)
+        inner = 128 * jnp.bitwise_and(lane, 7) + jnp.bitwise_and(lane, -8) + b
+        return place.c * COLS + jnp.where(b < NLB, inner, edge)
 
     def col_factor(b, carry):
         gc = col_of(b)
@@ -358,8 +376,8 @@
     tile_rows = slice(0, 128)
     wire.start(meas.at[:, :, last, :], meas.at[:, :, before, :], place.tile(1, 0), rim_group)
     wire.start(meas.at[:, :, first, :], meas.at[:, :, after, :], place.tile(-1, 0), rim_group)
-    for side, b, dc in ((0, 0, -1), (1, NLB - 1, 1)):
-        src, dst = meas.at[:, b], beside.at[side]
+    for side, dc in ((0, -1), (1, 1)):
+        src, dst = rims.at[side], beside.at[side]
         wire.start(src.at[:, tile_rows, :], dst.at[:, tile_rows, :], place.tile(0, dc), rim_group)
         wire.start(src.at[:, last, :], dst.at[:, before, :], place.tile(1, dc), rim_group)
         wire.start(src.at[:, first, :], dst.at[:, after, :], place.tile(-1, dc), rim_group)
@@ -372,7 +390,6 @@
 
     gc8 = col_of(NLB)
     col_in = jnp.where((gc8 >= 0) & (gc8 < TOTAL_COLS), 1.0, 0.0)
-    lane9 = lanes_of((NLB + 1, 8, 128))
 
     def scaled(m, amount):
         k = rowm[m] * amount
@@ -380,10 +397,15 @@
 
     def around(field, part, i):
         mid = field[part, i]
-        right = pltpu.roll(mid, 1, 2)
-        left = pltpu.roll(mid, 127, 2)
-        right = jnp.where(lane9 == 0, jnp.concatenate([right[NLB:], right[:NLB]], axis=0), right)
-        left = jnp.where(lane9 == 127, jnp.concatenate([left[1:], left[:1]], axis=0), left)
+        first, last, edge = mid[0], mid[NLB - 1], mid[NLB]
+        ahead = pltpu.roll(jnp.where(lane == 8, edge, first), 119, 1)
+        behind = pltpu.roll(jnp.where(lane == 119, edge, last), 9, 1)
+        right_last = jnp.where(lane < 120, pltpu.roll(first, 120, 1), ahead)
+        left_first = jnp.where(lane < 8, behind, pltpu.roll(last, 8, 1))
+        right_edge = jnp.where(lane == 119, ahead, pltpu.roll(edge, 127, 1))
+        left_edge = jnp.where(lane == 8, behind, pltpu.roll(edge, 1, 1))
+        right = jnp.concatenate([mid[1:NLB], right_last[None], right_edge[None]], axis=0)
+        left = jnp.concatenate([left_first[None], mid[: NLB - 1], left_edge[None]], axis=0)
         return (field[part, i - 1] + field[part, i + 1]) + (right + left)
 
     def wrap(field):
@@ -492,7 +514,11 @@
     for s in sums:
         s.middle_second()
     for s in sums:
-        s.end_second(out)
+        wire.arrived(s.r4)
+    for plane in (0, 1):
+        blocks = sums[0].end_second(plane) + sums[1].end_second(plane)
+        for b, block in enumerate(swapped(blocks)):
+            out[plane, :, 128 * b : 128 * (b + 1)] = block
     wire.all_sent()
 
 
@@ -502,9 +528,11 @@
     scratch = [
         pltpu.VMEM((2, EXT, COLS + 128), f32),
         pltpu.VMEM((2, 2, NLB + 1, EXT, 128), f32),
+        pltpu.VMEM((2, 8, COLS), f32),
         pltpu.VMEM((2, 2, 8, 128), f32),
         pltpu.VMEM((2, ROWS, COLS), jnp.bfloat16),
         pltpu.VMEM((2, NLB, EXT, 128), f32),
+        pltpu.VMEM((2, 2, ROWS, 128), f32),
         pltpu.VMEM((2, 2, EXT, 128), f32),
         field,
         field,

time: 61.4 us -> 58.4 us (0.951)
  Pallas kernels: 59.1 us -> 56.1 us
    pallas_call x1, Pallas kernels: 59.1 us -> 56.1 us  [per_device(): pl.pallas_call(kernel, out_shape=jax.ShapeDtypeStruct(phase_delay.shape,...]
where the time goes in v3:
time: 58.4 us; the launch traced here: 57.6 us
  Pallas kernels  56.1 us (96%)
  local copies, waits for them, and re-layouts  1.47 us (3%)
    pallas_call x1, Pallas kernels, per_device(): pl.pallas_call(kernel, out_shape=jax.ShapeDtypeStruct(phase_delay.shape,...  56.1 us
    unnamed x1, local copies, waits for them, and re-layouts  1.47 us

profile of v3, /device:TPU:32, one launch (start us, length us, event | category | flops | bytes accessed | tf_op | source)
XLA Modules:
  0.0 57.6 jit_solution(3250424207956962388)
XLA Ops:
  0.0 56.1 %tomography.1 = f32[2,8,1024]{2,1,0:T(8,128)} custom-call(f32[2,8,1024]{2,1,0:T(8,128)} %phase_hbm.1, s32[1,2]{1,0:T(1,128)} %angles.1, bf16[2,1,128,1024]{3,2,1,0:T(8,128)(2,1)} %meas_hbm.1), custom_call_target="tpu_custom_call" | custom-call | tf_op jit(solution)/shard_map/tomography/pallas_call | solution.py:564
  56.2 1.5 %copy.5 = f32[2,8,1024]{2,1,0:T(8,128)} copy(f32[2,8,1024]{2,1,0:T(8,128)} %tomography.1) | data formatting | bytes 131072

commit v4 on v3

--- a/solution.py
+++ b/solution.py
@@ -15,7 +15,7 @@
 AG_UNITS = ((0, 7, "zx"), (7, 9, "xz"))
 RS_UNITS = ((0, 6, "xz"), (6, 8, "zx"))
 N_SEM = 60
-UNROLL = 3
+UNROLL = 9
 SPAN = 720
 
 
@@ -81,129 +81,140 @@
 
 
 class Gather:
-    def __init__(self, wire, place, planes, trig, unit):
-        self.w, self.p, self.planes, self.trig = wire, place, planes, trig
+    def __init__(self, wire, place, planes, trig, plane, unit):
+        self.w, self.p, self.planes, self.trig, self.plane = wire, place, planes, trig, plane
         self.b0, self.b1, self.order = unit
-        self.lanes = slice(128 * self.b0, 128 * self.b1)
-        self.first = [wire.group() for _ in range(3)]
-        self.second = {da: [wire.group() for _ in range(2)] for da in (0, -1, 1, 2)}
+        self.mid = (self.b0 + self.b1) // 2
+        self.first = [wire.group() for _ in range(2)]
+        self.second = {da: wire.group() for da in (0, -1, 1, 2)}
         self.last = wire.group()
 
     def pos(self, da, db):
         return (da, db) if self.order == "zx" else (db, da)
 
-    def send(self, da, db, step, group, plane=None):
+    def send(self, da, db, step, group, half=None):
         rows = self.p.rows(*self.pos(da, db))
-        lead = slice(None) if plane is None else plane
-        ref = self.planes.at[lead, rows, self.lanes]
+        b0, b1 = ((self.b0, self.b1), (self.b0, self.mid), (self.mid, self.b1))[half or 0]
+        ref = self.planes.at[self.plane, rows, 128 * b0 : 128 * b1]
         self.w.start(ref, ref, self.p.illum(*self.pos(*step)), group)
 
-    def start_first(self):
+    def start(self):
         self.send(0, 0, (1, 0), self.first[0])
-        self.send(0, 0, (-1, 0), self.first[1])
-
-    def relay_first(self, way):
-        self.w.arrived(self.first[way])
-        if way == 0:
-            self.send(-1, 0, (1, 0), self.first[2], 0)
-        else:
-            self.send(1, 0, (-1, 0), self.first[2], 1)
+        self.send(0, 0, (-1, 0), self.first[0])
+        self.start_second(0)
+
+    def relay_first(self):
+        self.w.arrived(self.first[0])
+        self.send(-1, 0, (1, 0), self.first[1], 1)
+        self.send(1, 0, (-1, 0), self.first[1], 2)
+        self.start_second(-1)
+        self.start_second(1)
 
     def end_first(self):
-        self.w.arrived(self.first[2])
+        self.w.arrived(self.first[1])
+        self.start_second(2)
 
     def start_second(self, da):
-        self.send(da, 0, (0, 1), self.second[da][0])
-        self.send(da, 0, (0, -1), self.second[da][1])
-
-    def relay_second(self, da):
-        self.w.arrived(self.second[da][0])
-        self.send(da, -1, (0, 1), self.last, 0)
-        self.w.arrived(self.second[da][1])
-        self.send(da, 1, (0, -1), self.last, 1)
+        self.send(da, 0, (0, 1), self.second[da])
+        self.send(da, 0, (0, -1), self.second[da])
+
+    def relay_second(self, *das):
+        for da in das:
+            self.w.arrived(self.second[da])
+            self.send(da, -1, (0, 1), self.last, 1)
+            self.send(da, 1, (0, -1), self.last, 2)
 
     def end(self):
         self.w.arrived(self.last)
 
-    def turn(self, da, *dbs):
-        for db in dbs:
-            turn_rows(self.planes, self.trig, self.p.rows(*self.pos(da, db)), self.b0, self.b1)
-
-
-def turn_rows(planes, trig, rows, b0, b1):
-    s, c = sincos(planes[:, rows, 128 * b0 : 128 * b1])
+    def turn(self, das, dbs):
+        for da in das:
+            for db in dbs:
+                rows = self.p.rows(*self.pos(da, db))
+                turn_rows(self.planes, self.trig, self.plane, rows, self.b0, self.b1)
+
+
+def turn_rows(planes, trig, plane, rows, b0, b1):
+    s, c = sincos(planes[plane, rows, 128 * b0 : 128 * b1])
     for b in range(b0, b1):
         at = slice(128 * (b - b0), 128 * (b - b0 + 1))
-        for plane in (0, 1):
-            trig[plane, 0, b, rows, :] = c[plane, :, at]
-            trig[plane, 1, b, rows, :] = s[plane, :, at]
+        trig[plane, 0, b, rows, :] = c[:, at]
+        trig[plane, 1, b, rows, :] = s[:, at]
 
 
 class Scatter:
-    def __init__(self, wire, place, grads, unit, bufs):
-        self.w, self.p, self.g = wire, place, grads
+    def __init__(self, wire, place, grads, plane, unit, bufs):
+        self.w, self.p, self.g, self.plane = wire, place, grads, plane
         self.b0, self.b1, self.order = unit
+        self.n, self.h = self.b1 - self.b0, (self.b1 - self.b0) // 2
         self.t1, self.t2, self.sums, self.t3, self.t4 = bufs
-        self.r1 = {dq: (wire.group(), wire.group()) for dq in range(4)}
-        self.r2 = {dq: wire.group() for dq in range(4)}
-        self.r3 = (wire.group(), wire.group())
-        self.r4 = wire.group()
+        one, two = (wire.group() for _ in range(2))
+        self.r1 = {2: one, 1: one, 3: two, 0: two}
+        one, two = (wire.group() for _ in range(2))
+        self.r2 = {2: one, 1: one, 3: two, 0: two}
+        self.r3, self.r4 = wire.group(), wire.group()
 
     def pos(self, da, db):
         return (da, db) if self.order == "zx" else (db, da)
 
-    def part(self, da, dq, plane):
-        return (plane, slice(self.b0, self.b1), self.p.rows(*self.pos(da, dq)), slice(None))
+    def part(self, da, dq, half=0):
+        m = self.b0 + self.h
+        lanes = (slice(self.b0, self.b1), slice(self.b0, m), slice(m, self.b1))[half]
+        return (self.plane, lanes, self.p.rows(*self.pos(da, dq)), slice(None))
 
     def send(self, src, dst, da, db, group):
         self.w.start(src, dst, self.p.illum(*self.pos(da, db)), group)
 
     def start_first(self):
         for dq in (2, 1, 3, 0):
-            self.send(self.g.at[self.part(2, dq, 0)], self.t1.at[0, dq], 1, 0, self.r1[dq][0])
-            self.send(self.g.at[self.part(2, dq, 1)], self.t1.at[1, dq], -1, 0, self.r1[dq][1])
+            self.send(self.g.at[self.part(2, dq, 1)], self.t1.at[0, dq], 1, 0, self.r1[dq])
+            self.send(self.g.at[self.part(2, dq, 2)], self.t1.at[1, dq], -1, 0, self.r1[dq])
+
+    def early_first(self):
         for dq in (2, 1, 3, 0):
-            self.send(self.g.at[self.part(1, dq, 1)], self.t2.at[0, dq, 1], 1, 0, self.r2[dq])
-            self.send(self.g.at[self.part(-1, dq, 0)], self.t2.at[1, dq, 0], -1, 0, self.r2[dq])
+            self.send(self.g.at[self.part(1, dq, 2)], self.t2.at[0, dq, self.h :], 1, 0, self.r2[dq])
+            self.send(self.g.at[self.part(-1, dq, 1)], self.t2.at[1, dq, : self.h], -1, 0, self.r2[dq])
 
     def middle_first(self):
         for dq in (2, 1, 3, 0):
-            self.w.arrived(self.r1[dq][0])
-            at = self.part(1, dq, 0)
+            if dq in (2, 3):
+                self.w.arrived(self.r1[dq])
+            at = self.part(1, dq, 1)
             self.g[at] = self.g[at] + self.t1[0, dq]
-            self.send(self.g.at[at], self.t2.at[0, dq, 0], 1, 0, self.r2[dq])
-            self.w.arrived(self.r1[dq][1])
-            at = self.part(-1, dq, 1)
+            at = self.part(-1, dq, 2)
             self.g[at] = self.g[at] + self.t1[1, dq]
-            self.send(self.g.at[at], self.t2.at[1, dq, 1], -1, 0, self.r2[dq])
+        for dq in (2, 1, 3, 0):
+            self.send(self.g.at[self.part(1, dq, 1)], self.t2.at[0, dq, : self.h], 1, 0, self.r2[dq])
+            self.send(self.g.at[self.part(-1, dq, 2)], self.t2.at[1, dq, self.h :], -1, 0, self.r2[dq])
 
     def add_first(self, dq):
-        self.w.arrived(self.r2[dq])
-        for plane in (0, 1):
-            own = self.g[self.part(0, dq, plane)]
-            self.sums[dq, plane] = own + self.t2[0, dq, plane] + self.t2[1, dq, plane]
+        self.sums[dq] = self.g[self.part(0, dq)] + self.t2[0, dq] + self.t2[1, dq]
 
     def start_second(self):
+        h = self.h
+        self.w.arrived(self.r2[2])
         self.add_first(2)
-        self.send(self.sums.at[2, 0], self.t3.at[0], 0, 1, self.r3[0])
-        self.send(self.sums.at[2, 1], self.t3.at[1], 0, -1, self.r3[1])
         self.add_first(1)
-        self.send(self.sums.at[1, 1], self.t4.at[0, 1], 0, 1, self.r4)
+        self.send(self.sums.at[2, :h], self.t3.at[0], 0, 1, self.r3)
+        self.send(self.sums.at[2, h:], self.t3.at[1], 0, -1, self.r3)
+        self.w.arrived(self.r2[3])
         self.add_first(3)
-        self.send(self.sums.at[3, 0], self.t4.at[1, 0], 0, -1, self.r4)
+        self.send(self.sums.at[1, h:], self.t4.at[0, h:], 0, 1, self.r4)
+        self.send(self.sums.at[3, :h], self.t4.at[1, :h], 0, -1, self.r4)
         self.add_first(0)
 
     def middle_second(self):
-        self.w.arrived(self.r3[0])
-        self.sums[1, 0] = self.sums[1, 0] + self.t3[0]
-        self.send(self.sums.at[1, 0], self.t4.at[0, 0], 0, 1, self.r4)
-        self.w.arrived(self.r3[1])
-        self.sums[3, 1] = self.sums[3, 1] + self.t3[1]
-        self.send(self.sums.at[3, 1], self.t4.at[1, 1], 0, -1, self.r4)
-
-    def end_second(self, plane):
-        total = self.sums[0, plane] + self.t4[0, plane] + self.t4[1, plane]
-        return [total[b] for b in range(self.b1 - self.b0)]
+        h = self.h
+        self.w.arrived(self.r3)
+        self.sums[1, :h] = self.sums[1, :h] + self.t3[0]
+        self.sums[3, h:] = self.sums[3, h:] + self.t3[1]
+        self.send(self.sums.at[1, :h], self.t4.at[0, :h], 0, 1, self.r4)
+        self.send(self.sums.at[3, h:], self.t4.at[1, h:], 0, -1, self.r4)
+
+    def end_second(self):
+        self.w.arrived(self.r4)
+        total = self.sums[0] + self.t4[0] + self.t4[1]
+        return [total[b] for b in range(self.n)]
 
 
 def strided(m):
@@ -235,9 +246,9 @@
 def kernel(
     phase_hbm, angles, meas_hbm, out,
     planes, trig, fresh, edges, raw, meas, rims, beside, w0, w1, rim, adj, back1, rowf, colf, rowm, energy, energy_in,
-    grads, span, t1a, t2a, suma, t3a, t4a, t1b, t2b, sumb, t3b, t4b,
-    local, send, recv,
+    grads, span, *rest,
 ):
+    *bufs, local, send, recv = rest
     place = Place()
     wire = Wire(send, recv, span)
     own = place.rows(0, 0)
@@ -258,20 +269,20 @@
     edge_group = wire.group()
     wire.start(phase_hbm.at[:, :, :128], edges.at[0], place.tile(0, -1), edge_group)
     wire.start(phase_hbm.at[:, :, COLS - 128 :], edges.at[1], place.tile(0, 1), edge_group)
-    one = Gather(wire, place, planes, trig, AG_UNITS[0])
-    two = Gather(wire, place, planes, trig, AG_UNITS[1])
+    units = [[Gather(wire, place, planes, trig, plane, u) for u in AG_UNITS] for plane in (0, 1)]
+    (main0, side0), (main1, side1) = units
     fetch[0].wait()
     for b, block in enumerate(swapped(split(fresh[...]))):
         planes[:, own, 128 * b : 128 * (b + 1)] = block
-    one.start_first()
-    one.start_second(0)
-    one.turn(0, 0)
+    main0.start()
+    main1.start()
     wire.arrived(edge_group)
     lane = lanes_of((2, 8, 128))
     planes[:, own, COLS:] = jnp.where(lane < 64, pltpu.roll(edges[0], 8, 2), pltpu.roll(edges[1], 120, 2))
-    two.start_first()
-    two.start_second(0)
-    two.turn(0, 0)
+    side0.start()
+    side1.start()
+    main0.turn((0,), (0,))
+    main1.turn((0,), (0,))
 
     fetch[1].wait()
     energy[0] = jnp.zeros((8, 128), jnp.float32)
@@ -296,79 +307,76 @@
     lax.fori_loop(0, ROWS // 16, widen, 0)
 
     step_a, step_b = angles[0, 0], angles[0, 1]
-    sub = lax.broadcasted_iota(jnp.int32, (8, 128), 0)
-
-    def row_factor(m, carry):
-        r = sub * STEPS + m
-        gr = place.y * ROWS + jnp.where(r < 136, r, r - EXT)
-        inside = jnp.where((gr >= 0) & (gr < TOTAL_ROWS), 1.0, 0.0)
-        turns = jnp.bitwise_and(step_a * gr, TOTAL_ROWS - 1).astype(jnp.float32)
-        theta = turns * (2.0 * math.pi / TOTAL_ROWS)
-        co, si = jnp.cos(theta), jnp.sin(theta)
-        rowf[0, m] = inside * (-0.28 * co - 0.96 * si)
-        rowf[1, m] = inside * (0.96 * co - 0.28 * si)
-        rowm[m] = inside
-        return carry
-
     lane = lanes_of((8, 128))
+
+    def circle(steps, period):
+        turns = jnp.bitwise_and(steps + period // 2, period - 1) - period // 2
+        s, c = sincos(turns.astype(jnp.float32) * (0.5 * math.pi / period))
+        s, c = 2.0 * s * c, 1.0 - 2.0 * s * s
+        return 2.0 * s * c, 1.0 - 2.0 * s * s
 
     def col_of(b):
         edge = jnp.where(lane < 64, COLS - 8 + lane, lane - 120)
         inner = 128 * jnp.bitwise_and(lane, 7) + jnp.bitwise_and(lane, -8) + b
-        return place.c * COLS + jnp.where(b < NLB, inner, edge)
-
-    def col_factor(b, carry):
-        gc = col_of(b)
+        return place.c * COLS + (inner if b < NLB else edge)
+
+    def factors():
+        shape = (STEPS, 8, 128)
+        r = lax.broadcasted_iota(jnp.int32, shape, 1) * STEPS + lax.broadcasted_iota(jnp.int32, shape, 0)
+        gr = place.y * ROWS + jnp.where(r < 136, r, r - EXT)
+        inside = jnp.where((gr >= 0) & (gr < TOTAL_ROWS), 1.0, 0.0)
+        si, co = circle(step_a * gr, TOTAL_ROWS)
+        rowf[0] = inside * (-0.28 * co - 0.96 * si)
+        rowf[1] = inside * (0.96 * co - 0.28 * si)
+        rowm[...] = inside
+        gc = jnp.stack([col_of(b) for b in range(NLB + 1)])
         inside = jnp.where((gc >= 0) & (gc < TOTAL_COLS), 1.0, 0.0)
-        turns = jnp.bitwise_and(step_b * gc, TOTAL_COLS - 1).astype(jnp.float32)
-        theta = turns * (2.0 * math.pi / TOTAL_COLS)
-        colf[0, b] = inside * jnp.cos(theta)
-        colf[1, b] = inside * jnp.sin(theta)
-        return carry
-
-    one.relay_second(0)
-    one.turn(0, -1, 1)
-    two.relay_first(0)
-    two.start_second(-1)
-    two.relay_first(1)
-    two.start_second(1)
-    lax.fori_loop(0, STEPS, row_factor, 0)
-    lax.fori_loop(0, NLB + 1, col_factor, 0)
-    one.relay_first(0)
-    one.start_second(-1)
-    one.relay_first(1)
-    one.start_second(1)
-    one.turn(-1, 0)
-    one.turn(1, 0)
-    two.turn(-1, 0)
-    two.turn(1, 0)
-    two.end_first()
-    two.start_second(2)
-    two.turn(2, 0)
-    two.relay_second(0)
-    two.turn(0, -1, 1)
-    one.relay_second(-1)
-    one.turn(-1, -1, 1)
-    one.relay_second(1)
-    one.turn(1, -1, 1)
-    one.end_first()
-    one.start_second(2)
-    one.turn(2, 0)
-    two.relay_second(-1)
-    two.turn(-1, -1, 1)
-    two.relay_second(1)
-    two.turn(1, -1, 1)
-    two.relay_second(2)
-    two.turn(2, -1, 1)
-    one.relay_second(2)
-    one.turn(2, -1, 1)
-    two.end()
-    one.end()
-    end_group = wire.group()
+        si, co = circle(step_b * gc, TOTAL_COLS)
+        colf[0] = inside * co
+        colf[1] = inside * si
+
+    main0.relay_second(0)
+    side0.relay_first()
+    main1.relay_second(0)
+    side1.relay_first()
+    main0.relay_first()
+    side0.end_first()
+    side1.end_first()
+    main0.turn((0,), (-1, 1))
+    main0.turn((-1, 1), (0,))
+    factors()
+    main1.relay_first()
+    side0.relay_second(0)
+    main0.end_first()
+    main0.relay_second(-1, 1)
+    side1.relay_second(0)
+    side0.relay_second(-1, 1)
+    main1.end_first()
+    main0.turn((-1, 1), (-1, 1))
+    main0.turn((2,), (0,))
+    side0.relay_second(2)
+    main0.relay_second(2)
+    main1.relay_second(-1, 1)
+    side0.turn((0, -1, 1, 2), (0, -1, 1))
+    side1.relay_second(-1, 1, 2)
+
     last, first = slice(120, 128), slice(0, 8)
     after, before = slice(128, 136), slice(136, 144)
-    wire.start(planes.at[:, last, :], planes.at[:, before, :], place.tile(1, 0), end_group)
-    wire.start(planes.at[:, first, :], planes.at[:, after, :], place.tile(-1, 0), end_group)
+    end_groups = [wire.group(), wire.group()]
+
+    def share_ends(plane):
+        ref = planes.at[plane]
+        for unit in units[plane]:
+            unit.end()
+        wire.start(ref.at[last, :], ref.at[before, :], place.tile(1, 0), end_groups[plane])
+        wire.start(ref.at[first, :], ref.at[after, :], place.tile(-1, 0), end_groups[plane])
+
+    def turn_ends(plane):
+        wire.arrived(end_groups[plane])
+        turn_rows(planes, trig, plane, slice(128, 144), 0, NLB + 1)
+
+    share_ends(0)
+    main1.relay_second(2)
     energy_group = wire.group()
     for d in (1, 2, 3):
         wire.start(energy.at[0], energy_in.at[d - 1], place.tile(d, 0), energy_group)
@@ -381,12 +389,14 @@
         wire.start(src.at[:, tile_rows, :], dst.at[:, tile_rows, :], place.tile(0, dc), rim_group)
         wire.start(src.at[:, last, :], dst.at[:, before, :], place.tile(1, dc), rim_group)
         wire.start(src.at[:, first, :], dst.at[:, after, :], place.tile(-1, dc), rim_group)
-    for unit in (one, two):
-        for da in (0, -1, 1, 2):
-            unit.turn(da, 2)
-    wire.arrived(end_group)
-    turn_rows(planes, trig, after, 0, NLB + 1)
-    turn_rows(planes, trig, before, 0, NLB + 1)
+    main0.turn((2,), (-1, 1))
+    main0.turn((0, -1, 1, 2), (2,))
+    side0.turn((0, -1, 1, 2), (2,))
+    main1.turn((0,), (-1, 1))
+    main1.turn((-1, 1), (-1, 0, 1))
+    main1.turn((2,), (0,))
+    side1.turn((0, -1, 1, 2), (0, -1, 1))
+    turn_ends(0)
 
     gc8 = col_of(NLB)
     col_in = jnp.where((gc8 >= 0) & (gc8 < TOTAL_COLS), 1.0, 0.0)
@@ -445,8 +455,13 @@
         wrap(rim)
 
     sweep(enter)
+    share_ends(1)
     wrap(w0)
     first_sweep(w0, 0.5)
+    main1.turn((2,), (-1, 1))
+    main1.turn((0, -1, 1, 2), (2,))
+    side1.turn((0, -1, 1, 2), (2,))
+    turn_ends(1)
 
     def between(i):
         ur, ui = add_around(w0, rim, i, 0.2)
@@ -493,6 +508,14 @@
         back1[1, i] = gi * co - gr * si
 
     sweep(back)
+    late, early = (
+        [Scatter(wire, place, grads, plane, u, bufs[5 * k : 5 * k + 5]) for k, u in pairs]
+        for plane, pairs in ((0, tuple(enumerate(RS_UNITS))), (1, tuple(enumerate(RS_UNITS, 2))))
+    )
+    for s in early:
+        s.start_first()
+    for s in early:
+        s.early_first()
     wrap(back1)
     first_sweep(back1, -0.5)
 
@@ -503,20 +526,24 @@
 
     sweep(finish)
 
-    bufs = ((t1a, t2a, suma, t3a, t4a), (t1b, t2b, sumb, t3b, t4b))
-    sums = [Scatter(wire, place, grads, unit, b) for unit, b in zip(RS_UNITS, bufs)]
-    for s in sums:
+    for s in late:
         s.start_first()
-    for s in sums:
+    for s in early:
         s.middle_first()
-    for s in sums:
+    for s in late:
+        s.early_first()
+    for s in late:
+        s.middle_first()
+    for s in early:
         s.start_second()
-    for s in sums:
+    for s in late:
+        s.start_second()
+    for s in early:
         s.middle_second()
-    for s in sums:
-        wire.arrived(s.r4)
-    for plane in (0, 1):
-        blocks = sums[0].end_second(plane) + sums[1].end_second(plane)
+    for s in late:
+        s.middle_second()
+    for plane, parts in ((1, early), (0, late)):
+        blocks = [block for s in parts for block in s.end_second()]
         for b, block in enumerate(swapped(blocks)):
             out[plane, :, 128 * b : 128 * (b + 1)] = block
     wire.all_sent()
@@ -547,14 +574,14 @@
         pltpu.VMEM((2, NLB, EXT, 128), f32),
         pltpu.VMEM((SPAN, 8, 128), f32),
     ]
-    for b0, b1, _ in RS_UNITS:
+    for b0, b1, _ in RS_UNITS * 2:
         n = b1 - b0
         scratch += [
+            pltpu.VMEM((2, 4, n // 2, 8, 128), f32),
             pltpu.VMEM((2, 4, n, 8, 128), f32),
-            pltpu.VMEM((2, 4, 2, n, 8, 128), f32),
-            pltpu.VMEM((4, 2, n, 8, 128), f32),
+            pltpu.VMEM((4, n, 8, 128), f32),
+            pltpu.VMEM((2, n // 2, 8, 128), f32),
             pltpu.VMEM((2, n, 8, 128), f32),
-            pltpu.VMEM((2, 2, n, 8, 128), f32),
         ]
     scratch += [
         pltpu.SemaphoreType.DMA((2,)),

time: 58.4 us -> 58.7 us (level); the launches traced: 57.6 us -> 58.6 us
  Pallas kernels: 56.1 us -> 57.1 us
    pallas_call x1, Pallas kernels: 56.1 us -> 57.1 us  [per_device(): pl.pallas_call(kernel, out_shape=jax.ShapeDtypeStruct(phase_delay.shape,...]
where the time goes in v4:
time: 58.7 us; the launch traced here: 58.6 us
  Pallas kernels  57.1 us (97%)
  local copies, waits for them, and re-layouts  1.47 us (3%)
    pallas_call x1, Pallas kernels, per_device(): pl.pallas_call(kernel, out_shape=jax.ShapeDtypeStruct(phase_delay.shape,...  57.1 us
    unnamed x1, local copies, waits for them, and re-layouts  1.47 us

profile of v4, /device:TPU:32, one launch (start us, length us, event | category | flops | bytes accessed | tf_op | source)
XLA Modules:
  0.0 58.6 jit_solution(1290221132008468027)
XLA Ops:
  0.0 57.1 %tomography.1 = f32[2,8,1024]{2,1,0:T(8,128)} custom-call(f32[2,8,1024]{2,1,0:T(8,128)} %phase_hbm.1, s32[1,2]{1,0:T(1,128)} %angles.1, bf16[2,1,128,1024]{3,2,1,0:T(8,128)(2,1)} %meas_hbm.1), custom_call_target="tpu_custom_call" | custom-call | tf_op jit(solution)/shard_map/tomography/pallas_call | solution.py:591
  57.1 1.5 %copy.5 = f32[2,8,1024]{2,1,0:T(8,128)} copy(f32[2,8,1024]{2,1,0:T(8,128)} %tomography.1) | data formatting | bytes 131072

commit v5 on v4

--- a/solution.py
+++ b/solution.py
@@ -12,9 +12,10 @@
 TOTAL_ROWS, TOTAL_COLS = 512, 4096
 EPS_ENERGY = 1e-06
 MESH = pl.DeviceIdType.MESH
-AG_UNITS = ((0, 7, "zx"), (7, 9, "xz"))
+AG_UNITS = ((0, 6, "zx", True, True), (6, 8, "xz", False, True))
+HALO_UNIT = (8, 9, "zx", False, False)
 RS_UNITS = ((0, 6, "xz"), (6, 8, "zx"))
-N_SEM = 60
+N_SEM = 62
 UNROLL = 9
 SPAN = 720
 
@@ -83,11 +84,12 @@
 class Gather:
     def __init__(self, wire, place, planes, trig, plane, unit):
         self.w, self.p, self.planes, self.trig, self.plane = wire, place, planes, trig, plane
-        self.b0, self.b1, self.order = unit
+        self.b0, self.b1, self.order, *self.relays = unit
         self.mid = (self.b0 + self.b1) // 2
-        self.first = [wire.group() for _ in range(2)]
+        self.first = [wire.group() for _ in range(1 + self.relays[0])]
         self.second = {da: wire.group() for da in (0, -1, 1, 2)}
-        self.last = wire.group()
+        if self.relays[1]:
+            self.last = wire.group()
 
     def pos(self, da, db):
         return (da, db) if self.order == "zx" else (db, da)
@@ -95,18 +97,24 @@
     def send(self, da, db, step, group, half=None):
         rows = self.p.rows(*self.pos(da, db))
         b0, b1 = ((self.b0, self.b1), (self.b0, self.mid), (self.mid, self.b1))[half or 0]
-        ref = self.planes.at[self.plane, rows, 128 * b0 : 128 * b1]
+        lead = slice(None) if self.plane is None else self.plane
+        ref = self.planes.at[lead, rows, 128 * b0 : 128 * b1]
         self.w.start(ref, ref, self.p.illum(*self.pos(*step)), group)
 
     def start(self):
         self.send(0, 0, (1, 0), self.first[0])
         self.send(0, 0, (-1, 0), self.first[0])
+        if not self.relays[0]:
+            self.send(0, 0, (2, 0), self.first[0])
         self.start_second(0)
 
     def relay_first(self):
         self.w.arrived(self.first[0])
-        self.send(-1, 0, (1, 0), self.first[1], 1)
-        self.send(1, 0, (-1, 0), self.first[1], 2)
+        if self.relays[0]:
+            self.send(-1, 0, (1, 0), self.first[1], 1)
+            self.send(1, 0, (-1, 0), self.first[1], 2)
+        else:
+            self.start_second(2)
         self.start_second(-1)
         self.start_second(1)
 
@@ -117,12 +125,15 @@
     def start_second(self, da):
         self.send(da, 0, (0, 1), self.second[da])
         self.send(da, 0, (0, -1), self.second[da])
+        if not self.relays[1]:
+            self.send(da, 0, (0, 2), self.second[da])
 
     def relay_second(self, *das):
         for da in das:
             self.w.arrived(self.second[da])
-            self.send(da, -1, (0, 1), self.last, 1)
-            self.send(da, 1, (0, -1), self.last, 2)
+            if self.relays[1]:
+                self.send(da, -1, (0, 1), self.last, 1)
+                self.send(da, 1, (0, -1), self.last, 2)
 
     def end(self):
         self.w.arrived(self.last)
@@ -131,7 +142,8 @@
         for da in das:
             for db in dbs:
                 rows = self.p.rows(*self.pos(da, db))
-                turn_rows(self.planes, self.trig, self.plane, rows, self.b0, self.b1)
+                for plane in (0, 1) if self.plane is None else (self.plane,):
+                    turn_rows(self.planes, self.trig, plane, rows, self.b0, self.b1)
 
 
 def turn_rows(planes, trig, plane, rows, b0, b1):
@@ -257,6 +269,7 @@
         pltpu.make_async_copy(meas_hbm.at[:, 0], raw, local.at[1]),
     ]
     partners = [place.illum(1, 0), place.illum(-1, 0), place.illum(0, 1), place.illum(0, -1)]
+    partners += [place.illum(2, 0), place.illum(0, 2)]
     partners += [place.tile(d, 0) for d in (1, 2, 3)] + [place.tile(0, d) for d in (1, 2, 3)]
     partners += [place.tile(d, e) for d in (1, -1) for e in (1, -1)]
     barrier = pltpu.get_barrier_semaphore()
@@ -271,18 +284,18 @@
     wire.start(phase_hbm.at[:, :, COLS - 128 :], edges.at[1], place.tile(0, 1), edge_group)
     units = [[Gather(wire, place, planes, trig, plane, u) for u in AG_UNITS] for plane in (0, 1)]
     (main0, side0), (main1, side1) = units
+    halo = Gather(wire, place, planes, trig, None, HALO_UNIT)
     fetch[0].wait()
     for b, block in enumerate(swapped(split(fresh[...]))):
         planes[:, own, 128 * b : 128 * (b + 1)] = block
     main0.start()
+    side0.start()
     main1.start()
+    side1.start()
     wire.arrived(edge_group)
     lane = lanes_of((2, 8, 128))
     planes[:, own, COLS:] = jnp.where(lane < 64, pltpu.roll(edges[0], 8, 2), pltpu.roll(edges[1], 120, 2))
-    side0.start()
-    side1.start()
-    main0.turn((0,), (0,))
-    main1.turn((0,), (0,))
+    halo.start()
 
     fetch[1].wait()
     energy[0] = jnp.zeros((8, 128), jnp.float32)
@@ -305,6 +318,9 @@
         return carry
 
     lax.fori_loop(0, ROWS // 16, widen, 0)
+    energy_group = wire.group()
+    for d in (1, 2, 3):
+        wire.start(energy.at[0], energy_in.at[d - 1], place.tile(d, 0), energy_group)
 
     step_a, step_b = angles[0, 0], angles[0, 1]
     lane = lanes_of((8, 128))
@@ -335,30 +351,39 @@
         colf[0] = inside * co
         colf[1] = inside * si
 
+    every, near = (0, -1, 1, 2), (0, -1, 1)
     main0.relay_second(0)
     side0.relay_first()
     main1.relay_second(0)
     side1.relay_first()
+    main0.turn((0,), near)
     main0.relay_first()
-    side0.end_first()
-    side1.end_first()
-    main0.turn((0,), (-1, 1))
+    halo.turn((0,), (0,))
+    halo.relay_first()
+    side0.turn(every, (0,))
+    main1.relay_first()
+    wire.arrived(energy_group)
+    energy[1] = energy[0] + energy_in[0] + energy_in[1] + energy_in[2]
+    energy_group = wire.group()
+    for d in (1, 2, 3):
+        wire.start(energy.at[1], energy_in.at[2 + d], place.tile(0, d), energy_group)
+    factors()
     main0.turn((-1, 1), (0,))
-    factors()
-    main1.relay_first()
     side0.relay_second(0)
     main0.end_first()
+    side0.relay_second(-1, 1)
     main0.relay_second(-1, 1)
     side1.relay_second(0)
-    side0.relay_second(-1, 1)
     main1.end_first()
+    side0.relay_second(2)
+    side1.relay_second(-1, 1)
     main0.turn((-1, 1), (-1, 1))
     main0.turn((2,), (0,))
-    side0.relay_second(2)
     main0.relay_second(2)
     main1.relay_second(-1, 1)
-    side0.turn((0, -1, 1, 2), (0, -1, 1))
-    side1.relay_second(-1, 1, 2)
+    side1.relay_second(2)
+    side0.turn(every, (-1, 1))
+    halo.relay_second(*every)
 
     last, first = slice(120, 128), slice(0, 8)
     after, before = slice(128, 136), slice(136, 144)
@@ -377,9 +402,6 @@
 
     share_ends(0)
     main1.relay_second(2)
-    energy_group = wire.group()
-    for d in (1, 2, 3):
-        wire.start(energy.at[0], energy_in.at[d - 1], place.tile(d, 0), energy_group)
     rim_group = wire.group()
     tile_rows = slice(0, 128)
     wire.start(meas.at[:, :, last, :], meas.at[:, :, before, :], place.tile(1, 0), rim_group)
@@ -390,12 +412,13 @@
         wire.start(src.at[:, last, :], dst.at[:, before, :], place.tile(1, dc), rim_group)
         wire.start(src.at[:, first, :], dst.at[:, after, :], place.tile(-1, dc), rim_group)
     main0.turn((2,), (-1, 1))
-    main0.turn((0, -1, 1, 2), (2,))
-    side0.turn((0, -1, 1, 2), (2,))
-    main1.turn((0,), (-1, 1))
-    main1.turn((-1, 1), (-1, 0, 1))
+    main0.turn(every, (2,))
+    side0.turn(every, (2,))
+    halo.turn((0,), (-1, 1, 2))
+    halo.turn((-1, 1, 2), every)
+    main1.turn(near, near)
     main1.turn((2,), (0,))
-    side1.turn((0, -1, 1, 2), (0, -1, 1))
+    side1.turn(every, near)
     turn_ends(0)
 
     gc8 = col_of(NLB)
@@ -459,8 +482,8 @@
     wrap(w0)
     first_sweep(w0, 0.5)
     main1.turn((2,), (-1, 1))
-    main1.turn((0, -1, 1, 2), (2,))
-    side1.turn((0, -1, 1, 2), (2,))
+    main1.turn(every, (2,))
+    side1.turn(every, (2,))
     turn_ends(1)
 
     def between(i):
@@ -471,11 +494,6 @@
         w1[1, i] = ur * si + ui * co
 
     sweep(between)
-    wire.arrived(energy_group)
-    energy[1] = energy[0] + energy_in[0] + energy_in[1] + energy_in[2]
-    energy_group = wire.group()
-    for d in (1, 2, 3):
-        wire.start(energy.at[1], energy_in.at[2 + d], place.tile(0, d), energy_group)
     wrap(w1)
     first_sweep(w1, 0.5)
 
@@ -547,6 +565,7 @@
         for b, block in enumerate(swapped(blocks)):
             out[plane, :, 128 * b : 128 * (b + 1)] = block
     wire.all_sent()
+    assert len(wire.groups) <= N_SEM
 
 
 def per_device(phase_delay, angles, measured):

time: 58.7 us -> 55.8 us (0.951)
  Pallas kernels: 57.1 us -> 53.7 us
    pallas_call x1, Pallas kernels: 57.1 us -> 53.7 us  [per_device(): pl.pallas_call(kernel, out_shape=jax.ShapeDtypeStruct(phase_delay.shape,...]
where the time goes in v5:
time: 55.8 us; the launch traced here: 55.2 us
  Pallas kernels  53.7 us (96%)
  local copies, waits for them, and re-layouts  1.47 us (3%)
    pallas_call x1, Pallas kernels, per_device(): pl.pallas_call(kernel, out_shape=jax.ShapeDtypeStruct(phase_delay.shape,...  53.7 us
    unnamed x1, local copies, waits for them, and re-layouts  1.47 us

profile of v5, /device:TPU:32, one launch (start us, length us, event | category | flops | bytes accessed | tf_op | source)
XLA Modules:
  0.0 55.2 jit_solution(7545099836736058761)
XLA Ops:
  0.0 53.7 %tomography.1 = f32[2,8,1024]{2,1,0:T(8,128)} custom-call(f32[2,8,1024]{2,1,0:T(8,128)} %phase_hbm.1, s32[1,2]{1,0:T(1,128)} %angles.1, bf16[2,1,128,1024]{3,2,1,0:T(8,128)(2,1)} %meas_hbm.1), custom_call_target="tpu_custom_call" | custom-call | tf_op jit(solution)/shard_map/tomography/pallas_call | solution.py:610
  53.7 1.5 %copy.5 = f32[2,8,1024]{2,1,0:T(8,128)} copy(f32[2,8,1024]{2,1,0:T(8,128)} %tomography.1) | data formatting | bytes 131072

commit v6 on v5

--- a/solution.py
+++ b/solution.py
@@ -13,9 +13,9 @@
 EPS_ENERGY = 1e-06
 MESH = pl.DeviceIdType.MESH
 AG_UNITS = ((0, 6, "zx", True, True), (6, 8, "xz", False, True))
-HALO_UNIT = (8, 9, "zx", False, False)
+HALO_UNIT = (8, 9, "zx", True, False)
 RS_UNITS = ((0, 6, "xz"), (6, 8, "zx"))
-N_SEM = 62
+N_SEM = 64
 UNROLL = 9
 SPAN = 720
 
@@ -97,7 +97,9 @@
     def send(self, da, db, step, group, half=None):
         rows = self.p.rows(*self.pos(da, db))
         b0, b1 = ((self.b0, self.b1), (self.b0, self.mid), (self.mid, self.b1))[half or 0]
-        lead = slice(None) if self.plane is None else self.plane
+        lead = self.plane
+        if lead is None:
+            lead, b0, b1 = (half - 1 if half else slice(None)), self.b0, self.b1
         ref = self.planes.at[lead, rows, 128 * b0 : 128 * b1]
         self.w.start(ref, ref, self.p.illum(*self.pos(*step)), group)
 
@@ -269,8 +271,8 @@
         pltpu.make_async_copy(meas_hbm.at[:, 0], raw, local.at[1]),
     ]
     partners = [place.illum(1, 0), place.illum(-1, 0), place.illum(0, 1), place.illum(0, -1)]
-    partners += [place.illum(2, 0), place.illum(0, 2)]
-    partners += [place.tile(d, 0) for d in (1, 2, 3)] + [place.tile(0, d) for d in (1, 2, 3)]
+    partners.append(place.illum(0, 2))
+    partners += [place.tile(d, 0) for d in (1, -1)] + [place.tile(0, d) for d in (1, 2, 3)]
     partners += [place.tile(d, e) for d in (1, -1) for e in (1, -1)]
     barrier = pltpu.get_barrier_semaphore()
     for device in partners:
@@ -319,8 +321,13 @@
 
     lax.fori_loop(0, ROWS // 16, widen, 0)
     energy_group = wire.group()
-    for d in (1, 2, 3):
-        wire.start(energy.at[0], energy_in.at[d - 1], place.tile(d, 0), energy_group)
+    wire.start(energy.at[0], energy_in.at[0], place.tile(1, 0), energy_group)
+    wire.start(energy.at[0], energy_in.at[1], place.tile(-1, 0), energy_group)
+    rim_group = wire.group()
+    tile_rows, last, first = slice(0, 128), slice(120, 128), slice(0, 8)
+    after, before = slice(128, 136), slice(136, 144)
+    wire.start(meas.at[:, :, last, :], meas.at[:, :, before, :], place.tile(1, 0), rim_group)
+    wire.start(meas.at[:, :, first, :], meas.at[:, :, after, :], place.tile(-1, 0), rim_group)
 
     step_a, step_b = angles[0, 0], angles[0, 1]
     lane = lanes_of((8, 128))
@@ -352,41 +359,45 @@
         colf[1] = inside * si
 
     every, near = (0, -1, 1, 2), (0, -1, 1)
+    every, near = (0, -1, 1, 2), (0, -1, 1)
     main0.relay_second(0)
+    main0.turn((0,), near)
+    main0.relay_first()
     side0.relay_first()
     main1.relay_second(0)
+    wire.arrived(energy_group)
+    far_group = wire.group()
+    wire.start(energy_in.at[0], energy_in.at[2], place.tile(1, 0), far_group)
+    halo.turn((0,), (0,))
+    main1.relay_first()
     side1.relay_first()
-    main0.turn((0,), near)
-    main0.relay_first()
-    halo.turn((0,), (0,))
+    main0.turn((-1, 1), (0,))
     halo.relay_first()
+    factors()
     side0.turn(every, (0,))
-    main1.relay_first()
-    wire.arrived(energy_group)
+    side0.relay_second(0)
+    main0.end_first()
+    main0.relay_second(-1, 1)
+    side1.relay_second(0)
+    halo.end_first()
+    main1.end_first()
+    side0.relay_second(-1, 1)
+    main1.relay_second(-1, 1)
+    wire.arrived(far_group)
     energy[1] = energy[0] + energy_in[0] + energy_in[1] + energy_in[2]
     energy_group = wire.group()
     for d in (1, 2, 3):
         wire.start(energy.at[1], energy_in.at[2 + d], place.tile(0, d), energy_group)
-    factors()
-    main0.turn((-1, 1), (0,))
-    side0.relay_second(0)
-    main0.end_first()
-    side0.relay_second(-1, 1)
-    main0.relay_second(-1, 1)
-    side1.relay_second(0)
-    main1.end_first()
     side0.relay_second(2)
     side1.relay_second(-1, 1)
     main0.turn((-1, 1), (-1, 1))
     main0.turn((2,), (0,))
     main0.relay_second(2)
-    main1.relay_second(-1, 1)
     side1.relay_second(2)
+    main1.relay_second(2)
     side0.turn(every, (-1, 1))
     halo.relay_second(*every)
 
-    last, first = slice(120, 128), slice(0, 8)
-    after, before = slice(128, 136), slice(136, 144)
     end_groups = [wire.group(), wire.group()]
 
     def share_ends(plane):
@@ -401,11 +412,6 @@
         turn_rows(planes, trig, plane, slice(128, 144), 0, NLB + 1)
 
     share_ends(0)
-    main1.relay_second(2)
-    rim_group = wire.group()
-    tile_rows = slice(0, 128)
-    wire.start(meas.at[:, :, last, :], meas.at[:, :, before, :], place.tile(1, 0), rim_group)
-    wire.start(meas.at[:, :, first, :], meas.at[:, :, after, :], place.tile(-1, 0), rim_group)
     for side, dc in ((0, -1), (1, 1)):
         src, dst = rims.at[side], beside.at[side]
         wire.start(src.at[:, tile_rows, :], dst.at[:, tile_rows, :], place.tile(0, dc), rim_group)

time: 55.8 us -> 54.6 us (0.978)
  Pallas kernels: 53.7 us -> 53 us
    pallas_call x1, Pallas kernels: 53.7 us -> 53 us  [per_device(): pl.pallas_call(kernel, out_shape=jax.ShapeDtypeStruct(phase_delay.shape,...]
where the time goes in v6:
time: 54.6 us; the launch traced here: 54.5 us
  Pallas kernels  53 us (97%)
  local copies, waits for them, and re-layouts  1.47 us (3%)
    pallas_call x1, Pallas kernels, per_device(): pl.pallas_call(kernel, out_shape=jax.ShapeDtypeStruct(phase_delay.shape,...  53 us
    unnamed x1, local copies, waits for them, and re-layouts  1.47 us

profile of v6, /device:TPU:32, one launch (start us, length us, event | category | flops | bytes accessed | tf_op | source)
XLA Modules:
  0.0 54.5 jit_solution(10349418312297482430)
XLA Ops:
  0.0 53.0 %tomography.1 = f32[2,8,1024]{2,1,0:T(8,128)} custom-call(f32[2,8,1024]{2,1,0:T(8,128)} %phase_hbm.1, s32[1,2]{1,0:T(1,128)} %angles.1, bf16[2,1,128,1024]{3,2,1,0:T(8,128)(2,1)} %meas_hbm.1), custom_call_target="tpu_custom_call" | custom-call | tf_op jit(solution)/shard_map/tomography/pallas_call | solution.py:616
  53.0 1.5 %copy.5 = f32[2,8,1024]{2,1,0:T(8,128)} copy(f32[2,8,1024]{2,1,0:T(8,128)} %tomography.1) | data formatting | bytes 131072

commit v7 on v6

--- a/solution.py
+++ b/solution.py
@@ -14,9 +14,9 @@
 MESH = pl.DeviceIdType.MESH
 AG_UNITS = ((0, 6, "zx", True, True), (6, 8, "xz", False, True))
 HALO_UNIT = (8, 9, "zx", True, False)
-RS_UNITS = ((0, 6, "xz"), (6, 8, "zx"))
+RS_UNITS = ((0, 5, "xz"), (5, 8, "zx"))
 N_SEM = 64
-UNROLL = 9
+UNROLL = 18
 SPAN = 720
 
 
@@ -181,8 +181,8 @@
 
     def start_first(self):
         for dq in (2, 1, 3, 0):
-            self.send(self.g.at[self.part(2, dq, 1)], self.t1.at[0, dq], 1, 0, self.r1[dq])
-            self.send(self.g.at[self.part(2, dq, 2)], self.t1.at[1, dq], -1, 0, self.r1[dq])
+            self.send(self.g.at[self.part(2, dq, 1)], self.t1.at[0, dq, : self.h], 1, 0, self.r1[dq])
+            self.send(self.g.at[self.part(2, dq, 2)], self.t1.at[1, dq, : self.n - self.h], -1, 0, self.r1[dq])
 
     def early_first(self):
         for dq in (2, 1, 3, 0):
@@ -194,9 +194,9 @@
             if dq in (2, 3):
                 self.w.arrived(self.r1[dq])
             at = self.part(1, dq, 1)
-            self.g[at] = self.g[at] + self.t1[0, dq]
+            self.g[at] = self.g[at] + self.t1[0, dq, : self.h]
             at = self.part(-1, dq, 2)
-            self.g[at] = self.g[at] + self.t1[1, dq]
+            self.g[at] = self.g[at] + self.t1[1, dq, : self.n - self.h]
         for dq in (2, 1, 3, 0):
             self.send(self.g.at[self.part(1, dq, 1)], self.t2.at[0, dq, : self.h], 1, 0, self.r2[dq])
             self.send(self.g.at[self.part(-1, dq, 2)], self.t2.at[1, dq, self.h :], -1, 0, self.r2[dq])
@@ -209,8 +209,8 @@
         self.w.arrived(self.r2[2])
         self.add_first(2)
         self.add_first(1)
-        self.send(self.sums.at[2, :h], self.t3.at[0], 0, 1, self.r3)
-        self.send(self.sums.at[2, h:], self.t3.at[1], 0, -1, self.r3)
+        self.send(self.sums.at[2, :h], self.t3.at[0, :h], 0, 1, self.r3)
+        self.send(self.sums.at[2, h:], self.t3.at[1, : self.n - h], 0, -1, self.r3)
         self.w.arrived(self.r2[3])
         self.add_first(3)
         self.send(self.sums.at[1, h:], self.t4.at[0, h:], 0, 1, self.r4)
@@ -220,8 +220,8 @@
     def middle_second(self):
         h = self.h
         self.w.arrived(self.r3)
-        self.sums[1, :h] = self.sums[1, :h] + self.t3[0]
-        self.sums[3, h:] = self.sums[3, h:] + self.t3[1]
+        self.sums[1, :h] = self.sums[1, :h] + self.t3[0, :h]
+        self.sums[3, h:] = self.sums[3, h:] + self.t3[1, : self.n - h]
         self.send(self.sums.at[1, :h], self.t4.at[0, :h], 0, 1, self.r4)
         self.send(self.sums.at[3, h:], self.t4.at[1, h:], 0, -1, self.r4)
 
@@ -602,10 +602,10 @@
     for b0, b1, _ in RS_UNITS * 2:
         n = b1 - b0
         scratch += [
-            pltpu.VMEM((2, 4, n // 2, 8, 128), f32),
+            pltpu.VMEM((2, 4, n - n // 2, 8, 128), f32),
             pltpu.VMEM((2, 4, n, 8, 128), f32),
             pltpu.VMEM((4, n, 8, 128), f32),
-            pltpu.VMEM((2, n // 2, 8, 128), f32),
+            pltpu.VMEM((2, n - n // 2, 8, 128), f32),
             pltpu.VMEM((2, n, 8, 128), f32),
         ]
     scratch += [

time: 54.6 us -> 54.6 us (level)
  no operation moved by 1% of the time
where the time goes in v7:
time: 54.6 us; the launch traced here: 54.4 us
  Pallas kernels  53 us (97%)
  local copies, waits for them, and re-layouts  1.47 us (3%)
    pallas_call x1, Pallas kernels, per_device(): pl.pallas_call(kernel, out_shape=jax.ShapeDtypeStruct(phase_delay.shape,...  53 us
    unnamed x1, local copies, waits for them, and re-layouts  1.47 us

profile of v7, /device:TPU:32, one launch (start us, length us, event | category | flops | bytes accessed | tf_op | source)
XLA Modules:
  0.0 54.4 jit_solution(12270704516242784777)
XLA Ops:
  0.0 53.0 %tomography.1 = f32[2,8,1024]{2,1,0:T(8,128)} custom-call(f32[2,8,1024]{2,1,0:T(8,128)} %phase_hbm.1, s32[1,2]{1,0:T(1,128)} %angles.1, bf16[2,1,128,1024]{3,2,1,0:T(8,128)(2,1)} %meas_hbm.1), custom_call_target="tpu_custom_call" | custom-call | tf_op jit(solution)/shard_map/tomography/pallas_call | solution.py:616
  53.0 1.5 %copy.5 = f32[2,8,1024]{2,1,0:T(8,128)} copy(f32[2,8,1024]{2,1,0:T(8,128)} %tomography.1) | data formatting | bytes 131072

commit v8 on v7

--- a/solution.py
+++ b/solution.py
@@ -16,7 +16,7 @@
 HALO_UNIT = (8, 9, "zx", True, False)
 RS_UNITS = ((0, 5, "xz"), (5, 8, "zx"))
 N_SEM = 64
-UNROLL = 18
+UNROLL = 9
 SPAN = 720
 
 

time: 54.6 us -> 54.4 us (level)
  no operation moved by 1% of the time
where the time goes in v8:
time: 54.4 us; the launch traced here: 54.3 us
  Pallas kernels  52.8 us (97%)
  local copies, waits for them, and re-layouts  1.47 us (3%)
    pallas_call x1, Pallas kernels, per_device(): pl.pallas_call(kernel, out_shape=jax.ShapeDtypeStruct(phase_delay.shape,...  52.8 us
    unnamed x1, local copies, waits for them, and re-layouts  1.47 us

profile of v8, /device:TPU:32, one launch (start us, length us, event | category | flops | bytes accessed | tf_op | source)
XLA Modules:
  0.0 54.3 jit_solution(13478362640139076608)
XLA Ops:
  0.0 52.8 %tomography.1 = f32[2,8,1024]{2,1,0:T(8,128)} custom-call(f32[2,8,1024]{2,1,0:T(8,128)} %phase_hbm.1, s32[1,2]{1,0:T(1,128)} %angles.1, bf16[2,1,128,1024]{3,2,1,0:T(8,128)(2,1)} %meas_hbm.1), custom_call_target="tpu_custom_call" | custom-call | tf_op jit(solution)/shard_map/tomography/pallas_call | solution.py:616
  52.8 1.5 %copy.5 = f32[2,8,1024]{2,1,0:T(8,128)} copy(f32[2,8,1024]{2,1,0:T(8,128)} %tomography.1) | data formatting | bytes 131072
